TPU v7x, 32 devices: a whole 2x2x4 slice. The times are simulated.
32 devices in a mesh: region: 4 (over y, x), worker: 8 (over z, core).
Axes of the slice: x: 2, y: 2, z: 4, core: 2. Of those that a mesh axis runs over, the one named last changes fastest.
Arguments:
- worker_start: bfloat16 [4, 128, 4096], P('region'), may hold values from -0.5 to 0.5
- inputs: bfloat16 [4, 8, 4, 256, 128], P('region', 'worker'), may hold values from -6 to 6
- teacher: bfloat16 [128, 4096], replicated, may hold values from -0.5 to 0.5
- regional_momentum: float32 [4, 128, 4096], P('region', 'worker'), may hold values from -1.5 to 1.5
- global_params: float32 [128, 4096], P('worker', 'region'), may hold values from -6 to 6
- global_momentum: float32 [128, 4096], P('worker', 'region'), may hold values from -1.5 to 1.5
- staleness: int32 [4], replicated, may hold values from 0 to 4
- arrival_order: int32 [4], replicated, may hold values from 0 to 3, as said below
- pull_slot: int32 [4], replicated, may hold values from 0 to 3, as said below
Outputs:
- momentum_regional: float32 [4, 128, 4096], P('region', 'worker')
- params_global: float32 [128, 4096], P('worker', 'region')
- momentum_global: float32 [128, 4096], P('worker', 'region')
- worker_params: float32 [4, 128, 4096], P('region')
Inputs may be any that keep to these rules, and one draw needn't show every extreme that they name: arrival_order is a permutation of the regions 0 .. 3. pull_slot[r] is at least the position of region r in arrival_order; the region that arrives first has slot 0.
All inputs are finite; a program needn't handle non-finite values.
Results may differ from a plain program's by a relative error of at most 0.00043.
Values sent between devices are 32-bit elements; how exact they have to be, the bound alone decides.
No kernel may reach another device: no remote copies, remote signals or barrier semaphores. Data moves between devices by JAX's collectives and lax.ppermute only.
A program may use at most 64 MiB of HBM per device.

v0:
```python
import jax
import jax.numpy as jnp
from jax import lax
from jax.sharding import PartitionSpec as P

LOCAL_RATE = 0.3
REGION_BETA = 0.9
REGION_RATE = 1.0
GLOBAL_MU = 0.9
GLOBAL_RATE = 0.7


def residual_of(weights, micro_batch, teacher):
    target = jax.nn.silu(jnp.dot(micro_batch, teacher, preferred_element_type=jnp.float32))
    predicted = jnp.dot(
        micro_batch, weights.astype(jnp.bfloat16), preferred_element_type=jnp.float32
    )
    return (predicted - target).astype(jnp.bfloat16)


def gradient_of(micro_batch, residual):
    return lax.dot_general(
        micro_batch, residual, (((0,), (0,)), ((), ())), preferred_element_type=jnp.float32
    )


def merge_arrivals(deltas, region_dim, params_now, momentum_now, weights, arrival_order):

    def advance(state_pair, arrival):
        params_cur, momentum_cur = state_pair
        source = arrival_order[arrival]
        update = weights[source] * lax.dynamic_index_in_dim(
            deltas, source, region_dim, keepdims=False
        )
        momentum_cur = GLOBAL_MU * momentum_cur + update
        params_cur = params_cur - GLOBAL_RATE * (update + GLOBAL_MU * momentum_cur)
        return ((params_cur, momentum_cur), params_cur)

    return lax.scan(
        advance, (params_now, momentum_now), jnp.arange(arrival_order.shape[0], dtype=jnp.int32)
    )


def local(
    worker_start,
    inputs,
    teacher,
    regional_momentum,
    global_params,
    global_momentum,
    staleness,
    arrival_order,
    pull_slot,
):
    initial = worker_start[0]
    hidden = inputs[0, 0]
    step_scale = LOCAL_RATE / hidden.shape[1]
    start_weights = initial.astype(jnp.float32)
    local_steps = hidden.shape[0]
    current = start_weights
    for local_step in range(local_steps):
        residual = residual_of(current, hidden[local_step], teacher)
        current = current - step_scale * gradient_of(hidden[local_step], residual)
    pseudo = start_weights - current
    summed = lax.psum_scatter(pseudo, "worker", scatter_dimension=0, tiled=True)
    momentum_new = REGION_BETA * regional_momentum[0] + summed / lax.axis_size("worker")
    regional_delta = REGION_RATE * momentum_new
    weights = 1.0 / (1.0 + staleness.astype(jnp.float32))
    gathered, params_all, momentum_all = (
        lax.all_gather(regional_delta[None], "region", axis=0, tiled=True),
        lax.all_gather(global_params, "region", axis=1, tiled=True),
        lax.all_gather(global_momentum, "region", axis=1, tiled=True),
    )
    (params_full, momentum_full), versions = merge_arrivals(
        gathered, 0, params_all, momentum_all, weights, arrival_order
    )
    region_index = lax.axis_index("region")
    pulled_rows = lax.dynamic_index_in_dim(versions, pull_slot[region_index], 0, keepdims=False)
    columns = global_params.shape[1]
    params_out = lax.dynamic_slice_in_dim(params_full, region_index * columns, columns, 1)
    momentum_out = lax.dynamic_slice_in_dim(momentum_full, region_index * columns, columns, 1)
    worker_params = lax.all_gather(pulled_rows, "worker", axis=0, tiled=True)
    return (momentum_new[None], params_out, momentum_out, worker_params[None])


def solution(mesh):
    placed = (
        P("region", None, None),
        P("region", "worker", None, None, None),
        P(),
        P("region", "worker", None),
        P("worker", "region"),
        P("worker", "region"),
        P(),
        P(),
        P(),
    )
    return jax.shard_map(
        local,
        mesh=mesh,
        in_specs=placed,
        out_specs=(
            P("region", "worker", None),
            P("worker", "region"),
            P("worker", "region"),
            P("region", None, None),
        ),
        check_vma=False,
    )
```

profile of v0, /device:TPU:0, one launch (start us, length us, event | category | flops | bytes accessed | tf_op | source)
XLA Modules:
  0.0 192.3 jit_solution(16757103152995199145)
XLA Ops:
  8.4 3.5 %fusion.38 = f32[256,4096]{1,0:T(8,128)} fusion(bf16[128,4096]{1,0:T(8,128)(2,1)S(1)} %copy-done, bf16[1,1,4,256,128]{4,3,2,1,0:T(8,128)(2,1)} %param.12), kind=kOutput, calls=%fused_computation.44 | convolution fusion | flops 268435456 | bytes 5308416 | tf_op jit(solution)/shard_map/dot_general | solution.py:14
  11.9 2.7 %fusion.34 = f32[256,4096]{1,0:T(8,128)} fusion(bf16[128,4096]{1,0:T(8,128)(2,1)S(1)} %copy-done, bf16[1,1,4,256,128]{4,3,2,1,0:T(8,128)(2,1)S(1)} %copy-done.4), kind=kOutput, calls=%fused_computation.41 | convolution fusion | flops 268435456 | bytes 5308416 | tf_op jit(solution)/shard_map/dot_general | solution.py:14
  14.5 2.7 %fusion.30 = f32[256,4096]{1,0:T(8,128)} fusion(bf16[128,4096]{1,0:T(8,128)(2,1)S(1)} %copy-done, bf16[1,1,4,256,128]{4,3,2,1,0:T(8,128)(2,1)S(1)} %copy-done.4), kind=kOutput, calls=%fused_computation.38 | convolution fusion | flops 268435456 | bytes 5308416 | tf_op jit(solution)/shard_map/dot_general | solution.py:14
  17.2 2.6 %fusion.26 = f32[256,4096]{1,0:T(8,128)} fusion(bf16[128,4096]{1,0:T(8,128)(2,1)S(1)} %copy-done, bf16[1,1,4,256,128]{4,3,2,1,0:T(8,128)(2,1)S(1)} %copy-done.4), kind=kOutput, calls=%fused_computation.35 | convolution fusion | flops 268435456 | bytes 5308416 | tf_op jit(solution)/shard_map/dot_general | solution.py:14
  20.5 6.0 %fusion.17 = f32[128,4096]{0,1:T(8,128)} fusion(f32[256,4096]{1,0:T(8,128)} %fusion.38, bf16[1,128,4096]{2,1,0:T(8,128)(2,1)S(1)} %copy-done.1, bf16[1,128,4096]{1,2,0:T(8,128)(2,1)S(1)} %copy.22, bf16[1,1,4,256,128]{4,3,2,1,0:T(8,128)(2,1)S(1)} %copy-done.4), kind=kOutput, calls=%fused_computation.29 | convolution fusion | flops 544735232 | bytes 8519680 | tf_op jit(solution)/shard_map/dot_general | solution.py:22
  26.5 6.9 %fusion.15 = f32[128,4096]{0,1:T(8,128)} fusion(f32[128,4096]{0,1:T(8,128)} %fusion.17, f32[256,4096]{1,0:T(8,128)} %fusion.34, bf16[1,1,4,256,128]{4,3,2,1,0:T(8,128)(2,1)S(1)} %copy-done.4), kind=kOutput, calls=%fused_computation.26 | convolution fusion | flops 544735232 | bytes 10616832 | tf_op jit(solution)/shard_map/dot_general | solution.py:22
  33.3 6.8 %fusion.13 = f32[128,4096]{0,1:T(8,128)} fusion(f32[128,4096]{0,1:T(8,128)} %fusion.15, f32[256,4096]{1,0:T(8,128)} %fusion.30, bf16[1,1,4,256,128]{4,3,2,1,0:T(8,128)(2,1)S(1)} %copy-done.4), kind=kOutput, calls=%fused_computation.23 | convolution fusion | flops 544735232 | bytes 10616832 | tf_op jit(solution)/shard_map/dot_general | solution.py:22
  40.2 5.7 %fusion.11 = f32[128,4096]{0,1:T(8,128)S(1)} fusion(f32[128,4096]{0,1:T(8,128)} %fusion.13, f32[256,4096]{1,0:T(8,128)} %fusion.26, bf16[1,128,4096]{1,2,0:T(8,128)(2,1)} %copy-done.2, bf16[1,1,4,256,128]{4,3,2,1,0:T(8,128)(2,1)S(1)} %copy-done.4), kind=kOutput, calls=%fused_computation.20 | convolution fusion | flops 545783808 | bytes 11665408 | tf_op jit(solution)/shard_map/dot_general | solution.py:22
  45.9 1.8 copy.31
  48.7 2.0 %copy.21 = f32[1,16,4096]{1,2,0:T(8,128)} copy(f32[1,16,4096]{2,1,0:T(8,128)S(1)} %copy-done.3) | data formatting | bytes 524288 | tf_op args[3]
  50.6 36.0 %reduce-scatter.4.cloned.1.call-done = f32[16,4096]{1,0:T(8,128)} async-done(((f32[128,4096]{1,0:T(8,128)}), f32[16,4096]{1,0:T(8,128)}) %reduce-scatter.4.cloned.1.call-update) | async-done | bytes 262160
  86.6 2.9 %copy.32 = f32[16,4096]{0,1:T(8,128)} copy(f32[16,4096]{1,0:T(8,128)} %reduce-scatter.4.cloned.1.call-done) | data formatting | bytes 524288
  89.5 2.5 %bitcast_add_fusion.2 = f32[16,4096]{0,1:T(8,128)S(1)} fusion(f32[16,4096]{0,1:T(8,128)} %copy.32, f32[1,16,4096]{1,2,0:T(8,128)} %copy.21), kind=kLoop, calls=%fused_computation.30 | loop fusion | flops 196608 | bytes 786432 | tf_op jit(solution)/shard_map/add | solution.py:66
  96.0 10.2 %all_gather.12 = f32[16,4096]{1,0:T(8,128)S(1)} all-gather(f32[16,1024]{1,0:T(8,128)S(1)} %copy-done.5), channel_id=1, replica_groups=mesh['region'=4,'worker'=8] {'region'}, dimensions={1}, use_global_device_ids=true | all-gather | bytes 327680 | tf_op jit(solution)/shard_map/all_gather | solution.py:71
  106.2 11.1 %all_gather.13 = f32[16,4096]{1,0:T(8,128)} all-gather(f32[16,1024]{1,0:T(8,128)S(1)} %copy-done.6), channel_id=1, replica_groups=mesh['region'=4,'worker'=8] {'region'}, dimensions={1}, use_global_device_ids=true | all-gather | bytes 327680 | tf_op jit(solution)/shard_map/all_gather | solution.py:72
  117.4 2.0 %all-gather.5.cloned.1.call-done = f32[64,4096]{1,0:T(8,128)} async-done(((f32[16,4096]{1,0:T(8,128)}), f32[64,4096]{1,0:T(8,128)}) %all-gather.5.cloned.1.call-update) | async-done | bytes 1048592 | tf_op jit(solution)/shard_map/all_gather | solution.py:70
  119.3 33.0 %while.14 = (s32[]{:T(128)}, f32[16,4096]{1,0:T(8,128)S(1)}, f32[16,4096]{1,0:T(8,128)}, f32[4,16,4096]{2,1,0:T(8,128)}, s32[4]{0:T(128)S(1)}, /*index=5*/s32[4]...) while((s32[]{:T(128)}, f32[16,4096]{1,0:T(8,128)S(1)}, ...), condition=%wide.region_2.3_spmd, body=%wide.region_1.2_spmd.sunk | while | flops 458760 | bytes 1573605 | solution.py:39
  125.0 2.6 %bitcast_dynamic-update-slice_fusion.2 = (f32[4,16,4096]{2,1,0:T(8,128)}, f32[16,4096]{1,0:T(8,128)S(1)}, f32[16,4096]{1,0:T(8,128)}) fusion(f32[4,16,4096]{2,1,0:T(8,128)} %get-tuple-element.161, s32[]{:T(128)S(6)} %copy.38, f32[16,4096]{1,0:T(8,128)S(1)} %get-tuple-element.159, f32[4,16,4096]{2,1,0:T(8,128)} %get-tuple-element.176, s32[]{:T(128)S(6)} %select_n.24, ...), kind=kLoop, calls=%fused_computation.clone.1 | loop fusion | flops 458752 | bytes 1573384 | tf_op jit(solution)/shard_map/while/body/jit(dynamic_update_index_in_dim)/dynamic_update_slice | solution.py:39
  133.2 2.6 %bitcast_dynamic-update-slice_fusion.2 = (f32[4,16,4096]{2,1,0:T(8,128)}, f32[16,4096]{1,0:T(8,128)S(1)}, f32[16,4096]{1,0:T(8,128)}) fusion(f32[4,16,4096]{2,1,0:T(8,128)} %get-tuple-element.161, s32[]{:T(128)S(6)} %copy.38, f32[16,4096]{1,0:T(8,128)S(1)} %get-tuple-element.159, f32[4,16,4096]{2,1,0:T(8,128)} %get-tuple-element.176, s32[]{:T(128)S(6)} %select_n.24, ...), kind=kLoop, calls=%fused_computation.clone.1 | loop fusion | flops 458752 | bytes 1573384 | tf_op jit(solution)/shard_map/while/body/jit(dynamic_update_index_in_dim)/dynamic_update_slice | solution.py:39
  141.5 2.6 %bitcast_dynamic-update-slice_fusion.2 = (f32[4,16,4096]{2,1,0:T(8,128)}, f32[16,4096]{1,0:T(8,128)S(1)}, f32[16,4096]{1,0:T(8,128)}) fusion(f32[4,16,4096]{2,1,0:T(8,128)} %get-tuple-element.161, s32[]{:T(128)S(6)} %copy.38, f32[16,4096]{1,0:T(8,128)S(1)} %get-tuple-element.159, f32[4,16,4096]{2,1,0:T(8,128)} %get-tuple-element.176, s32[]{:T(128)S(6)} %select_n.24, ...), kind=kLoop, calls=%fused_computation.clone.1 | loop fusion | flops 458752 | bytes 1573384 | tf_op jit(solution)/shard_map/while/body/jit(dynamic_update_index_in_dim)/dynamic_update_slice | solution.py:39
  149.7 2.6 %bitcast_dynamic-update-slice_fusion.2 = (f32[4,16,4096]{2,1,0:T(8,128)}, f32[16,4096]{1,0:T(8,128)S(1)}, f32[16,4096]{1,0:T(8,128)}) fusion(f32[4,16,4096]{2,1,0:T(8,128)} %get-tuple-element.161, s32[]{:T(128)S(6)} %copy.38, f32[16,4096]{1,0:T(8,128)S(1)} %get-tuple-element.159, f32[4,16,4096]{2,1,0:T(8,128)} %get-tuple-element.176, s32[]{:T(128)S(6)} %select_n.24, ...), kind=kLoop, calls=%fused_computation.clone.1 | loop fusion | flops 458752 | bytes 1573384 | tf_op jit(solution)/shard_map/while/body/jit(dynamic_update_index_in_dim)/dynamic_update_slice | solution.py:39
  152.3 1.7 constant_dynamic-slice_fusion
  156.8 25.8 %all-gather.7.cloned.1.call-done = f32[1,128,4096]{2,1,0:T(8,128)} async-done(((f32[1,16,4096]{2,1,0:T(8,128)}), f32[1,128,4096]{2,1,0:T(8,128)}) %all-gather.7.cloned.1.call-update) | async-done | bytes 2097168 | tf_op jit(solution)/shard_map/all_gather | solution.py:82
  182.6 3.1 %copy.47 = f32[1,128,4096]{2,1,0:T(8,128)} copy(f32[1,128,4096]{2,1,0:T(8,128)} %all-gather.7.cloned.1.call-done) | data formatting | bytes 4194304
  (46 shorter events, 14.6 us)
Async XLA Ops:
  7.2 1.2 copy-start
  7.2 4.7 %copy-start.4 = (bf16[1,1,4,256,128]{4,3,2,1,0:T(8,128)(2,1)S(1)}, bf16[1,1,4,256,128]{4,3,2,1,0:T(8,128)(2,1)}, u32[]{:S(2)}) copy-start(bf16[1,1,4,256,128]{4,3,2,1,0:T(8,128)(2,1)} %param.12) | copy-start | bytes 786436
  7.2 79.4 %reduce-scatter.4.cloned.1.call-start = ((), (), s32[]{:S(2)}) async-start(), calls=%async_computation.3 | async-start | bytes 2359296
  17.2 2.7 %copy-start.1 = (bf16[1,128,4096]{2,1,0:T(8,128)(2,1)S(1)}, bf16[1,128,4096]{2,1,0:T(8,128)(2,1)}, u32[]{:S(2)}) copy-start(bf16[1,128,4096]{2,1,0:T(8,128)(2,1)} %param.11) | copy-start | bytes 3145732
  20.5 6.0 %copy-start.2 = (bf16[1,128,4096]{1,2,0:T(8,128)(2,1)}, bf16[1,128,4096]{1,2,0:T(8,128)(2,1)S(1)}, u32[]{:S(2)}) copy-start(bf16[1,128,4096]{1,2,0:T(8,128)(2,1)S(1)} %copy.22) | copy-start | bytes 3145732
  47.7 0.9 copy-start.3
  47.7 71.6 %all-gather.5.cloned.1.call-start = ((), (), s32[]{:S(2)}) async-start(), calls=%async_computation.1 | async-start | bytes 1310720 | tf_op jit(solution)/shard_map/all_gather | solution.py:70
  92.0 1.4 copy-start.7
  92.0 4.0 %copy-start.5 = (f32[16,1024]{1,0:T(8,128)S(1)}, f32[16,1024]{1,0:T(8,128)}, u32[]{:S(2)}) copy-start(f32[16,1024]{1,0:T(8,128)} %param.15) | copy-start | bytes 196612
  92.0 14.2 %copy-start.6 = (f32[16,1024]{1,0:T(8,128)S(1)}, f32[16,1024]{1,0:T(8,128)}, u32[]{:S(2)}) copy-start(f32[16,1024]{1,0:T(8,128)} %param.16) | copy-start | bytes 196612
  92.0 25.3 %copy-start.8 = (s32[4]{0:T(128)S(1)}, s32[4]{0:T(128)}, u32[]{:S(2)}) copy-start(s32[4]{0:T(128)} %param.17) | copy-start | bytes 52
  92.0 27.3 %copy-start.9 = (s32[4]{0:T(128)S(1)}, s32[4]{0:T(128)}, u32[]{:S(2)}) copy-start(s32[4]{0:T(128)} %param.18) | copy-start | bytes 52
  93.3 89.3 %all-gather.7.cloned.1.call-start = ((), (), s32[]{:S(2)}) async-start(), calls=%async_computation.2 | async-start | bytes 2359296 | tf_op jit(solution)/shard_map/all_gather | solution.py:82
Sparse Core Ops, SparseCore 0:
  47.8 38.7 reduce-scatter.3
  93.5 25.8 all-gather.4
  154.2 28.4 all-gather.6
where the time goes:
time: 193 us; the launch traced here: 192 us
  waiting for transfers between devices  63.8 us (33%)
  matrix products  36.8 us (19%)
  local copies, waits for them, and re-layouts  25.6 us (13%)
  blocking collectives  21.4 us (11%)
  between operations  15.8 us (8%)
  loops' own time  15.6 us (8%)
  other arithmetic  12.9 us (7%)
    unnamed x4, waiting for transfers between devices  36 us
    all_gather x1, waiting for transfers between devices, local(): worker_params = lax.all_gather(pulled_rows, 'worker', axis=0, tiled=True)  25.8 us
    dot_general x4, matrix products, gradient_of(): lax.dot_general(micro_batch, residual, (((0,), (0,)), ((), ())), preferre...  25.3 us
    another operation x1, loops' own time, merge_arrivals(): lax.scan(advance, (params_now, momentum_now), jnp.arange(arrival_order.sh...  15.6 us
    unnamed x26, local copies, waits for them, and re-layouts  13.6 us
    dot_general x4, matrix products, residual_of(): jnp.dot(micro_batch, teacher, preferred_element_type=jnp.float32)  11.5 us
    all_gather x1, blocking collectives, local(): lax.all_gather(global_momentum, 'region', axis=1, tiled=True)  11.1 us
    dynamic_update_slice x4, other arithmetic, merge_arrivals(): lax.scan(advance, (params_now, momentum_now), jnp.arange(arrival_order.sh...  10.4 us
  transfers between devices with their start and end apart: 3, of which 3 were waited for; matrix products, arithmetic and copies ran while one was open for 3% of the time, Pallas kernels for 0%

commit v1 on v0

v1 whole, which is shorter than its diff:
```python
import functools

import jax
import jax.numpy as jnp
from jax import lax
from jax.experimental import pallas as pl
from jax.experimental.pallas import tpu as pltpu
from jax.sharding import PartitionSpec as P

LOCAL_RATE = 0.3
REGION_BETA = 0.9
REGION_RATE = 1.0
GLOBAL_MU = 0.9
GLOBAL_RATE = 0.7

CHUNKS = 4
F32 = jnp.float32
BF16 = jnp.bfloat16
VMEM = pl.BlockSpec(memory_space=pltpu.VMEM)
SMEM = pl.BlockSpec(memory_space=pltpu.SMEM)
ANY = pl.BlockSpec(memory_space=pl.ANY)


def call(kernel, out, in_specs, out_specs, cost, name, **kwargs):
    flops, moved = cost
    return pl.pallas_call(
        kernel,
        out_shape=out,
        in_specs=in_specs,
        out_specs=out_specs,
        cost_estimate=pl.CostEstimate(flops=flops, bytes_accessed=moved, transcendentals=0),
        compiler_params=pltpu.CompilerParams(vmem_limit_bytes=16 * 1024 * 1024),
        name=name,
        **kwargs,
    )


def steps_kernel(offset, stride, pos_ref, x_ref, w_ref, t_ref, keep_ref, send_ref):
    core, chip = pos_ref[0], pos_ref[1]
    chips, strips, rows, width = keep_ref.shape
    local_steps, tokens, _ = x_ref.shape
    scale = LOCAL_RATE / tokens

    def columns(ref):
        return jnp.concatenate(
            [ref[:, s * stride + offset : s * stride + offset + width] for s in range(strips)], 1
        )

    start = columns(w_ref).astype(F32)
    half_teacher = (columns(t_ref).astype(F32) * 0.5).astype(BF16)

    def target(step):
        half = jnp.dot(x_ref[step], half_teacher, preferred_element_type=F32)
        return half + half * jnp.tanh(half)

    current = start
    wanted = target(0)
    for step in range(local_steps):
        x = x_ref[step]
        predicted = jnp.dot(x, current.astype(BF16), preferred_element_type=F32)
        residual = (predicted - wanted).astype(BF16)
        if step + 1 < local_steps:
            wanted = target(step + 1)
        gradient = lax.dot_general(
            x, residual, (((0,), (0,)), ((), ())), preferred_element_type=F32
        )
        current = current - scale * gradient
    pseudo = start - current
    for k in range(chips):
        slot = k ^ chip
        for s in range(strips):
            even = pseudo[2 * k * rows : (2 * k + 1) * rows, s * width : (s + 1) * width]
            odd = pseudo[(2 * k + 1) * rows : (2 * k + 2) * rows, s * width : (s + 1) * width]
            keep_ref[slot, s] = jnp.where(core == 0, even, odd)
            send_ref[slot, s] = jnp.where(core == 0, odd, even)


def add_kernel(keep_ref, got_ref, *out_refs):
    for k, out in enumerate(out_refs):
        out[...] = keep_ref[k] + got_ref[k]


def momentum_kernel(offset, stride, workers, *refs):
    *parts, old_ref, out_ref = refs
    strips, _, width = out_ref.shape
    for s in range(strips):
        total = parts[0][s]
        for part in parts[1:]:
            total = total + part[s]
        first = s * stride + offset
        out_ref[s] = REGION_RATE * (
            REGION_BETA * old_ref[:, first : first + width] + total / workers
        )


def merge_kernel(offset, regions, pos_ref, coef_ref, *refs):
    deltas, states = refs[:regions], refs[regions : 2 * regions]
    pulled_ref, params_ref, momentum_ref = refs[2 * regions :]
    me = pos_ref[2]
    width = pulled_ref.shape[2]
    for q in range(regions):
        strip = me ^ q
        params = states[q][0, :, offset : offset + width]
        momentum = states[q][1, :, offset : offset + width]
        terms = [deltas[p][strip] for p in range(regions)]
        pulled = params - coef_ref[0, regions] * momentum
        for p in range(regions):
            pulled = pulled - coef_ref[0, p] * terms[p]
        pulled_ref[strip] = pulled
        if q == 0:
            last = params - coef_ref[1, regions] * momentum
            carried = coef_ref[2, regions] * momentum
            for p in range(regions):
                last = last - coef_ref[1, p] * terms[p]
                carried = carried + coef_ref[2, p] * terms[p]
            params_ref[...] = last
            momentum_ref[...] = carried


def place_kernel(offset, stride, blocks, aliased, *refs):
    pos_ref, *rest = refs
    parts = rest[: blocks + 3]
    outs = rest[blocks + 3 + aliased : -1]
    sems = rest[-1]
    core, chip = pos_ref[0], pos_ref[1]
    pulled_ref, regional_ref, params_ref, momentum_ref = outs
    strips, _, width = parts[0].shape
    copies = []

    def copy(source, target):
        copies.append(pltpu.make_async_copy(source, target, sems.at[len(copies)]))
        copies[-1].start()

    for s in range(strips):
        columns = pl.ds(s * stride + offset, width)
        for b in range(blocks):
            owner = 2 * (chip ^ (b // 2)) + (core ^ (b % 2))
            copy(parts[b].at[s], pulled_ref.at[owner, :, columns])
        copy(parts[blocks].at[s], regional_ref.at[:, columns])
    copy(parts[blocks + 1], params_ref.at[:, pl.ds(offset, width)])
    copy(parts[blocks + 2], momentum_ref.at[:, pl.ds(offset, width)])
    for one in copies:
        one.wait()


def exchange(value, axis, bits):
    size = lax.axis_size(axis)
    return lax.ppermute(value, axis, [(i, i ^ bits) for i in range(size)])


def scatter_sum(blocks):
    bit, count = 1, len(blocks)
    while count > 4:
        got = exchange(jnp.stack(blocks[1::2]), "worker", 2 * bit)
        blocks = [b + got[i] for i, b in enumerate(blocks[0::2])]
        bit, count = 2 * bit, count // 2
    if count == 4:
        far = exchange(blocks[3], "worker", 2 * bit)
        near = exchange(blocks[1], "worker", 2 * bit)
        across = exchange(blocks[2] + far, "worker", 4 * bit)
        return [blocks[0], near, across]
    if count == 2:
        return [blocks[0], exchange(blocks[1], "worker", 2 * bit)]
    return blocks


def gather_blocks(block, chips):
    levels = chips.bit_length() - 1
    if levels >= 2:
        bit = chips // 4
        near = exchange(block, "worker", 2 * bit)
        across = exchange(block, "worker", 4 * bit)
        far = exchange(across, "worker", 2 * bit)
        blocks, bit = [block, near, across, far], bit // 2
    elif levels == 1:
        blocks, bit = [block, exchange(block, "worker", 2)], 0
    else:
        blocks, bit = [block], 0
    while bit >= 1:
        got = exchange(jnp.stack(blocks), "worker", 2 * bit)
        blocks = [part for i, b in enumerate(blocks) for part in (b, got[i])]
        bit //= 2
    return [part for b in blocks for part in (b, exchange(b, "worker", 1))]


def coefficients(staleness, arrival_order, pull_slot, region):
    count = arrival_order.shape[0]
    seen = jnp.arange(count, dtype=jnp.int32)
    relative = region ^ seen
    hits = arrival_order[None, :] == relative[:, None]
    position = jnp.sum(jnp.where(hits, seen[None, :], 0), axis=1)
    here = relative[:, None] == seen[None, :]
    stale = jnp.sum(jnp.where(here, staleness[None, :], 0), axis=1)
    slot = jnp.sum(jnp.where(seen == region, pull_slot, 0))
    weight = 1.0 / (1.0 + stale.astype(F32))
    step, own, carried = [], [], []
    total, power = 1.0, 1.0
    for _ in range(count):
        carried.append(power)
        power *= GLOBAL_MU
        total += power
        step.append(GLOBAL_RATE * total)
        own.append(GLOBAL_RATE * GLOBAL_MU * (total - 1.0))

    def pick(table, index):
        hit = index[..., None] == seen
        return jnp.sum(jnp.where(hit, jnp.array(table, F32), 0.0), axis=-1)

    last = count - 1
    deltas = jnp.stack(
        [pick(step, slot - position), pick(step, last - position), pick(carried, last - position)]
    )
    olds = jnp.stack([pick(own, slot), jnp.array(own[last], F32), jnp.array(power, F32)])
    return jnp.concatenate([deltas * weight[None, :], olds[:, None]], axis=1)


def local(
    worker_start,
    inputs,
    teacher,
    regional_momentum,
    global_params,
    global_momentum,
    staleness,
    arrival_order,
    pull_slot,
):
    initial, hidden, old = worker_start[0], inputs[0, 0], regional_momentum[0]
    depth, wide = initial.shape
    workers, regions = lax.axis_size("worker"), lax.axis_size("region")
    chips, rows, stride = workers // 2, depth // workers, wide // regions
    chunks = min(CHUNKS, stride // 128)
    width = stride // chunks
    region, worker = lax.axis_index("region"), lax.axis_index("worker")
    pos = jnp.stack([worker % 2, worker // 2, region]).astype(jnp.int32)
    coef = coefficients(staleness, arrival_order, pull_slot, region)
    state = jnp.stack([global_params, global_momentum])
    states = [state] + [exchange(state, "region", q) for q in range(1, regions)]

    block = jax.ShapeDtypeStruct((regions, rows, width), F32)
    strip = jax.ShapeDtypeStruct((rows, width), F32)
    half = jax.ShapeDtypeStruct((chips, regions, rows, width), F32)
    block_bytes = regions * rows * width * 4
    outs = None
    for j in range(chunks):
        offset = j * width
        keep, send = call(
            functools.partial(steps_kernel, offset, stride),
            (half, half),
            [SMEM, VMEM, VMEM, VMEM],
            (VMEM, VMEM),
            (6 * hidden.shape[0] * hidden.shape[1] * depth * width * regions, 2 * workers * block_bytes),
            f"steps_{j}",
        )(pos, hidden, initial, teacher)
        got = exchange(send, "worker", 1)
        blocks = call(
            add_kernel, (block,) * chips, [VMEM] * 2, (VMEM,) * chips,
            (0, 3 * chips * block_bytes), f"add_{j}",
        )(keep, got)
        parts = scatter_sum(blocks)
        delta = call(
            functools.partial(momentum_kernel, offset, stride, workers),
            block, [VMEM] * (len(parts) + 1), VMEM,
            (0, (len(parts) + 2) * block_bytes), f"momentum_{j}",
        )(*parts, old)
        deltas = [delta] + [exchange(delta, "region", q) for q in range(1, regions)]
        pulled, last, carried = call(
            functools.partial(merge_kernel, offset, regions),
            (block, strip, strip),
            [SMEM, SMEM] + [VMEM] * (2 * regions),
            (VMEM,) * 3,
            (0, (regions + 4) * block_bytes), f"merge_{j}",
        )(pos, coef, *deltas, *states)
        pieces = gather_blocks(pulled, chips) + [delta, last, carried]
        shapes = (
            jax.ShapeDtypeStruct((workers, rows, wide), F32),
            jax.ShapeDtypeStruct((rows, wide), F32),
            jax.ShapeDtypeStruct((rows, stride), F32),
            jax.ShapeDtypeStruct((rows, stride), F32),
        )
        before = () if outs is None else outs
        outs = call(
            functools.partial(place_kernel, offset, stride, workers, len(before)),
            shapes,
            [SMEM] + [VMEM] * len(pieces) + [ANY] * len(before),
            (ANY,) * 4,
            (0, 2 * workers * block_bytes), f"place_{j}",
            scratch_shapes=[pltpu.SemaphoreType.DMA((regions * (workers + 1) + 2,))],
            input_output_aliases={1 + len(pieces) + i: i for i in range(len(before))},
        )(pos, *pieces, *before)
    pulled, regional, params, momentum = outs
    return (regional[None], params, momentum, pulled.reshape(depth, wide)[None])


def solution(mesh):
    placed = (
        P("region", None, None),
        P("region", "worker", None, None, None),
        P(),
        P("region", "worker", None),
        P("worker", "region"),
        P("worker", "region"),
        P(),
        P(),
        P(),
    )
    return jax.shard_map(
        local,
        mesh=mesh,
        in_specs=placed,
        out_specs=(
            P("region", "worker", None),
            P("worker", "region"),
            P("worker", "region"),
            P("region", None, None),
        ),
        check_vma=False,
    )
```

time: 193 us -> 91.3 us (0.47)
  waiting for transfers between devices: 63.8 us -> 11.3 us
  starting transfers between devices: 0.3 us -> 51.7 us
  matrix products: 36.8 us -> 0 us
  local copies, waits for them, and re-layouts: 25.6 us -> 3.56 us
  blocking collectives: 21.4 us -> 0 us
  Pallas kernels: 0 us -> 19.6 us
  loops' own time: 15.6 us -> 0 us
  between operations: 15.8 us -> 1.1 us
  other arithmetic: 12.9 us -> 3.87 us
    ppermute x0 -> x59, starting transfers between devices: none -> 51.7 us  [exchange(): return lax.ppermute(value, axis, [(i, i ^ bits) for i in range(size)])]
    dot_general x8 -> x0, matrix products: 36.8 us -> none  [the longest x4 25.3 us: gradient_of(): lax.dot_general(micro_batch, residual, (((0,), (0,)), ((), ())), preferre...]
    unnamed x4 -> x0, waiting for transfers between devices: 36 us -> none
    all_gather x2 -> x0, waiting for transfers between devices: 27.8 us -> none  [the longest x1 25.8 us: local(): worker_params = lax.all_gather(pulled_rows, 'worker', axis=0, tiled=True)]
    all_gather x2 -> x0, blocking collectives: 21.4 us -> none  [the longest x1 11.1 us: local(): lax.all_gather(global_momentum, 'region', axis=1, tiled=True)]
    pallas_call x0 -> x20, Pallas kernels: none -> 19.6 us  [the longest x4 10.1 us: local(): call(functools.partial(steps_kernel, offset, stride), (half, half), [SMEM...]
    another operation x1 -> x0, loops' own time: 15.6 us -> none  [merge_arrivals(): lax.scan(advance, (params_now, momentum_now), jnp.arange(arrival_order.sh...]
    ppermute x0 -> x59, waiting for transfers between devices: none -> 11.3 us  [exchange(): return lax.ppermute(value, axis, [(i, i ^ bits) for i in range(size)])]
  transfers between devices with their start and end apart: 3 -> 59, of which waited for: 3 -> 7; matrix products, arithmetic and copies ran while one was open for 3% -> 4% of each run, Pallas kernels for 0% -> 17%
where the time goes in v1:
time: 91.3 us; the launch traced here: 91.1 us
  starting transfers between devices  51.7 us (57%)
  Pallas kernels  19.6 us (21%)
  waiting for transfers between devices  11.3 us (12%)
  other arithmetic  3.87 us (4%)
  local copies, waits for them, and re-layouts  3.56 us (4%)
  between operations  1.1 us (1%)
    ppermute x59, starting transfers between devices, exchange(): return lax.ppermute(value, axis, [(i, i ^ bits) for i in range(size)])  51.7 us
    ppermute x59, waiting for transfers between devices, exchange(): return lax.ppermute(value, axis, [(i, i ^ bits) for i in range(size)])  11.3 us
    pallas_call x4, Pallas kernels, local(): call(functools.partial(steps_kernel, offset, stride), (half, half), [SMEM...  10.1 us
    pallas_call x4, Pallas kernels, local(): call(functools.partial(place_kernel, offset, stride, workers, len(before)...  6.79 us
    unnamed x28, local copies, waits for them, and re-layouts  3.47 us
    pallas_call x4, Pallas kernels, local(): call(functools.partial(merge_kernel, offset, regions), (block, strip, str...  2.43 us
  transfers between devices with their start and end apart: 59, of which 7 were waited for; matrix products, arithmetic and copies ran while one was open for 4% of the time, Pallas kernels for 17%

profile of v1, /device:TPU:0, one launch (start us, length us, event | category | flops | bytes accessed | tf_op | source)
XLA Modules:
  0.0 91.1 jit_solution(865369091118973148)
XLA Ops:
  4.1 2.5 %steps_0.1 = (f32[4,4,16,256]{3,2,1,0:T(8,128)S(1)}, f32[4,4,16,256]{3,2,1,0:T(8,128)S(1)}) custom-call(s32[3]{0:T(128)S(1)} %pad_add_fusion.pos_ref.refs_0_, bf16[4,256,128]{2,1,0:T(8,128)(2,1)S(1)} %bitcast.24, bf16[128,4096]{1,0:T(8,128)(2,1)S(1)} %bitcast.20, bf16[128,4096]{1,0:T(8,128)(2,1)S(1)} %copy-done.2), custom_call_target="tpu_custom_call" | custom-call | flops 805306368 | bytes 1048576 | tf_op jit(solution)/shard_map/steps_0/pallas_call | solution.py:247
  7.2 2.5 %steps_1.1 = (f32[4,4,16,256]{3,2,1,0:T(8,128)S(1)}, f32[4,4,16,256]{3,2,1,0:T(8,128)S(1)}) custom-call(s32[3]{0:T(128)S(1)} %pad_add_fusion.pos_ref.refs_0_, bf16[4,256,128]{2,1,0:T(8,128)(2,1)S(1)} %bitcast.25, bf16[128,4096]{1,0:T(8,128)(2,1)S(1)} %bitcast.21, bf16[128,4096]{1,0:T(8,128)(2,1)S(1)} %copy-done.3), custom_call_target="tpu_custom_call" | custom-call | flops 805306368 | bytes 1048576 | tf_op jit(solution)/shard_map/steps_1/pallas_call | solution.py:247
  9.9 2.5 %steps_2.1 = (f32[4,4,16,256]{3,2,1,0:T(8,128)S(1)}, f32[4,4,16,256]{3,2,1,0:T(8,128)S(1)}) custom-call(s32[3]{0:T(128)S(1)} %pad_add_fusion.pos_ref.refs_0_, bf16[4,256,128]{2,1,0:T(8,128)(2,1)S(1)} %bitcast.26, bf16[128,4096]{1,0:T(8,128)(2,1)S(1)} %bitcast.22, bf16[128,4096]{1,0:T(8,128)(2,1)S(1)} %copy-done.3), custom_call_target="tpu_custom_call" | custom-call | flops 805306368 | bytes 1048576 | tf_op jit(solution)/shard_map/steps_2/pallas_call | solution.py:247
  13.1 2.5 %steps_3.1 = (f32[4,4,16,256]{3,2,1,0:T(8,128)S(1)}, f32[4,4,16,256]{3,2,1,0:T(8,128)S(1)}) custom-call(s32[3]{0:T(128)S(1)} %pad_add_fusion.pos_ref.refs_0_, bf16[4,256,128]{2,1,0:T(8,128)(2,1)S(1)} %bitcast.27, bf16[128,4096]{1,0:T(8,128)(2,1)S(1)} %bitcast.23, bf16[128,4096]{1,0:T(8,128)(2,1)S(1)} %copy-done.3), custom_call_target="tpu_custom_call" | custom-call | flops 805306368 | bytes 1048576 | tf_op jit(solution)/shard_map/steps_3/pallas_call | solution.py:247
  17.3 3.1 %collective-permute-start.47 = (f32[4,16,256]{2,1,0:T(8,128)S(1)}, f32[4,16,256]{2,1,0:T(8,128)S(1)}, u32[]{:S(2)}, u32[]{:S(2)}) collective-permute-start(f32[4,16,256]{2,1,0:T(8,128)S(1)} %get-tuple-element.88), channel_id=1, source_target_pairs={{0,2},{1,3},{2,0},{3,1},{4,6},{5,7},{6,4},{7,5},{8,10},{9,11},{10,... | collective-permute-start | bytes 196616 | tf_op jit(solution)/shard_map/ppermute | solution.py:148
  20.5 2.1 %collective-permute-start.33 = (f32[4,16,256]{2,1,0:T(8,128)S(1)}, f32[4,16,256]{2,1,0:T(8,128)S(1)}, u32[]{:S(2)}, u32[]{:S(2)}) collective-permute-start(f32[4,16,256]{2,1,0:T(8,128)S(1)} %get-tuple-element.79), channel_id=1, source_target_pairs={{0,2},{1,3},{2,0},{3,1},{4,6},{5,7},{6,4},{7,5},{8,10},{9,11},{10,... | collective-permute-start | bytes 196616 | tf_op jit(solution)/shard_map/ppermute | solution.py:148
  22.7 2.1 %collective-permute-start.2 = (f32[4,16,256]{2,1,0:T(8,128)S(1)}, f32[4,16,256]{2,1,0:T(8,128)S(1)}, u32[]{:S(2)}, u32[]{:S(2)}) collective-permute-start(f32[4,16,256]{2,1,0:T(8,128)S(1)} %get-tuple-element.61), channel_id=1, source_target_pairs={{0,2},{1,3},{2,0},{3,1},{4,6},{5,7},{6,4},{7,5},{8,10},{9,11},{10,... | collective-permute-start | bytes 196616 | tf_op jit(solution)/shard_map/ppermute | solution.py:148
  24.8 2.7 %collective-permute-start.48 = (f32[4,16,256]{2,1,0:T(8,128)S(1)}, f32[4,16,256]{2,1,0:T(8,128)S(1)}, u32[]{:S(2)}, u32[]{:S(2)}) collective-permute-start(f32[4,16,256]{2,1,0:T(8,128)S(1)} %add.29), channel_id=1, source_target_pairs={{0,4},{1,5},{2,6},{3,7},{4,0},{5,1},{6,2},{7,3},{8,12},{9,13},{10,... | collective-permute-start | bytes 196616 | tf_op jit(solution)/shard_map/ppermute | solution.py:148
  29.3 1.6 %collective-permute-start.8 = (f32[2,16,1024]{2,1,0:T(8,128)S(1)}, f32[2,16,1024]{2,1,0:T(8,128)S(1)}, u32[]{:S(2)}, u32[]{:S(2)}) collective-permute-start(f32[2,16,1024]{2,1,0:T(8,128)S(1)} %pad_maximum_fusion.refs_4_), channel_id=1, source_target_pairs={{0,16},{8,24},{16,0},{24,8},{1,17},{9,25},{17,1},{25,9},{2,18},{10... | collective-permute-start | bytes 393224 | tf_op jit(solution)/shard_map/ppermute | solution.py:148
  32.0 3.2 %collective-permute-start.34 = (f32[4,16,256]{2,1,0:T(8,128)S(1)}, f32[4,16,256]{2,1,0:T(8,128)S(1)}, u32[]{:S(2)}, u32[]{:S(2)}) collective-permute-start(f32[4,16,256]{2,1,0:T(8,128)S(1)} %add.28), channel_id=1, source_target_pairs={{0,4},{1,5},{2,6},{3,7},{4,0},{5,1},{6,2},{7,3},{8,12},{9,13},{10,... | collective-permute-start | bytes 196616 | tf_op jit(solution)/shard_map/ppermute | solution.py:148
  35.5 2.0 %collective-permute-start.1 = (f32[4,16,256]{2,1,0:T(8,128)S(1)}, f32[4,16,256]{2,1,0:T(8,128)S(1)}, u32[]{:S(2)}, u32[]{:S(2)}) collective-permute-start(f32[4,16,256]{2,1,0:T(8,128)S(1)} %get-tuple-element.59), channel_id=1, source_target_pairs={{0,2},{1,3},{2,0},{3,1},{4,6},{5,7},{6,4},{7,5},{8,10},{9,11},{10,... | collective-permute-start | bytes 196616 | tf_op jit(solution)/shard_map/ppermute | solution.py:148
  38.4 2.0 %collective-permute-start.3 = (f32[4,16,256]{2,1,0:T(8,128)S(1)}, f32[4,16,256]{2,1,0:T(8,128)S(1)}, u32[]{:S(2)}, u32[]{:S(2)}) collective-permute-start(f32[4,16,256]{2,1,0:T(8,128)S(1)} %add.26), channel_id=1, source_target_pairs={{0,4},{1,5},{2,6},{3,7},{4,0},{5,1},{6,2},{7,3},{8,12},{9,13},{10,... | collective-permute-start | bytes 196616 | tf_op jit(solution)/shard_map/ppermute | solution.py:148
  57.4 1.8 %collective-permute-start.55 = (f32[4,16,256]{2,1,0:T(8,128)S(1)}, f32[4,16,256]{2,1,0:T(8,128)S(1)}, u32[]{:S(2)}, u32[]{:S(2)}) collective-permute-start(f32[4,16,256]{2,1,0:T(8,128)S(1)} %get-tuple-element.89.refs_1_), channel_id=1, source_target_pairs={{0,4},{1,5},{2,6},{3,7},{4,0},{5,1},{6,2},{7,3},{8,12},{9,13},{10,... | collective-permute-start | bytes 196616 | tf_op jit(solution)/shard_map/ppermute | solution.py:148
  62.0 1.7 %collective-permute-start.39 = (f32[4,16,256]{2,1,0:T(8,128)S(1)}, f32[4,16,256]{2,1,0:T(8,128)S(1)}, u32[]{:S(2)}, u32[]{:S(2)}) collective-permute-start(f32[4,16,256]{2,1,0:T(8,128)S(1)} %get-tuple-element.80.refs_1_), channel_id=1, source_target_pairs={{0,2},{1,3},{2,0},{3,1},{4,6},{5,7},{6,4},{7,5},{8,10},{9,11},{10,... | collective-permute-start | bytes 196616 | tf_op jit(solution)/shard_map/ppermute | solution.py:148
  63.8 1.8 %collective-permute-start.27 = (f32[4,16,256]{2,1,0:T(8,128)S(1)}, f32[4,16,256]{2,1,0:T(8,128)S(1)}, u32[]{:S(2)}, u32[]{:S(2)}) collective-permute-start(f32[4,16,256]{2,1,0:T(8,128)S(1)} %get-tuple-element.71.refs_1_), channel_id=1, source_target_pairs={{0,4},{1,5},{2,6},{3,7},{4,0},{5,1},{6,2},{7,3},{8,12},{9,13},{10,... | collective-permute-start | bytes 196616 | tf_op jit(solution)/shard_map/ppermute | solution.py:148
  66.8 1.6 %collective-permute-done.41.refs_5_ = f32[4,16,256]{2,1,0:T(8,128)S(1)} collective-permute-done((f32[4,16,256]{2,1,0:T(8,128)S(1)}, f32[4,16,256]{2,1,0:T(8,128)S(1)}, u32[]{:S(2)}, u32[]{:S(2)}) %collective-permute-start.41) | collective-permute-done | bytes 65568 | tf_op jit(solution)/shard_map/ppermute | solution.py:148
  69.6 2.0 %collective-permute-start.11 = (f32[4,16,256]{2,1,0:T(8,128)S(1)}, f32[4,16,256]{2,1,0:T(8,128)S(1)}, u32[]{:S(2)}, u32[]{:S(2)}) collective-permute-start(f32[4,16,256]{2,1,0:T(8,128)S(1)} %get-tuple-element.62.refs_1_), channel_id=1, source_target_pairs={{0,2},{1,3},{2,0},{3,1},{4,6},{5,7},{6,4},{7,5},{8,10},{9,11},{10,... | collective-permute-start | bytes 196616 | tf_op jit(solution)/shard_map/ppermute | solution.py:148
  72.2 2.6 %collective-permute-done.13.refs_5_ = f32[4,16,256]{2,1,0:T(8,128)S(1)} collective-permute-done((f32[4,16,256]{2,1,0:T(8,128)S(1)}, f32[4,16,256]{2,1,0:T(8,128)S(1)}, u32[]{:S(2)}, u32[]{:S(2)}) %collective-permute-start.13) | collective-permute-done | bytes 65568 | tf_op jit(solution)/shard_map/ppermute | solution.py:148
  77.4 1.7 %collective-permute-done.43.refs_7_ = f32[4,16,256]{2,1,0:T(8,128)S(1)} collective-permute-done((f32[4,16,256]{2,1,0:T(8,128)S(1)}, f32[4,16,256]{2,1,0:T(8,128)S(1)}, u32[]{:S(2)}, u32[]{:S(2)}) %collective-permute-start.43) | collective-permute-done | bytes 65568 | tf_op jit(solution)/shard_map/ppermute | solution.py:148
  81.8 1.8 %collective-permute-done.15.refs_7_ = f32[4,16,256]{2,1,0:T(8,128)S(1)} collective-permute-done((f32[4,16,256]{2,1,0:T(8,128)S(1)}, f32[4,16,256]{2,1,0:T(8,128)S(1)}, u32[]{:S(2)}, u32[]{:S(2)}) %collective-permute-start.15) | collective-permute-done | bytes 65568 | tf_op jit(solution)/shard_map/ppermute | solution.py:148
  84.2 1.7 %place_0.1 = (f32[8,16,4096]{2,1,0:T(8,128)}, f32[16,4096]{1,0:T(8,128)}, f32[16,1024]{1,0:T(8,128)}, f32[16,1024]{1,0:T(8,128)}) custom-call(s32[3]{0:T(128)S(1)} %pad_add_fusion.pos_ref.refs_0_, f32[4,16,256]{2,1,0:T(8,128)S(1)} %get-tuple-element.89.refs_1_, f32[4,16,256]{2,1,0:T(8,128)S(1)} %collective-permute-done.52.refs_2_, ...), custom_call_target="tpu_custom_call" | custom-call | bytes 1048576 | tf_op jit(solution)/shard_map/place_0/pallas_call | solution.py:282
  85.9 1.7 %place_1.1 = (f32[8,16,4096]{2,1,0:T(8,128)}, f32[16,4096]{1,0:T(8,128)}, f32[16,1024]{1,0:T(8,128)}, f32[16,1024]{1,0:T(8,128)}) custom-call(s32[3]{0:T(128)S(1)} %pad_add_fusion.pos_ref.refs_0_, f32[4,16,256]{2,1,0:T(8,128)S(1)} %get-tuple-element.80.refs_1_, ...), custom_call_target="tpu_custom_call", output_to_operand_aliasing={{0}: (12, {}), {1}: (13, {}), {2}: (14, {}), {3}: (15, {})} | custom-call | bytes 1048576 | tf_op jit(solution)/shard_map/place_1/pallas_call | solution.py:282
  87.6 1.7 %place_2.1 = (f32[8,16,4096]{2,1,0:T(8,128)}, f32[16,4096]{1,0:T(8,128)}, f32[16,1024]{1,0:T(8,128)}, f32[16,1024]{1,0:T(8,128)}) custom-call(s32[3]{0:T(128)S(1)} %pad_add_fusion.pos_ref.refs_0_, f32[4,16,256]{2,1,0:T(8,128)S(1)} %get-tuple-element.71.refs_1_, ...), custom_call_target="tpu_custom_call", output_to_operand_aliasing={{0}: (12, {}), {1}: (13, {}), {2}: (14, {}), {3}: (15, {})} | custom-call | bytes 1048576 | tf_op jit(solution)/shard_map/place_2/pallas_call | solution.py:282
  89.4 1.7 %place_3.1 = (f32[8,16,4096]{2,1,0:T(8,128)}, f32[16,4096]{1,0:T(8,128)}, f32[16,1024]{1,0:T(8,128)}, f32[16,1024]{1,0:T(8,128)}) custom-call(s32[3]{0:T(128)S(1)} %pad_add_fusion.pos_ref.refs_0_, f32[4,16,256]{2,1,0:T(8,128)S(1)} %get-tuple-element.62.refs_1_, ...), custom_call_target="tpu_custom_call", output_to_operand_aliasing={{0}: (12, {}), {1}: (13, {}), {2}: (14, {}), {3}: (15, {})} | custom-call | bytes 1048576 | tf_op jit(solution)/shard_map/place_3/pallas_call | solution.py:282
  (158 shorter events, 39.3 us)
Async XLA Ops:
  6.7 10.5 %collective-permute-start.45 = (f32[4,4,16,256]{3,2,1,0:T(8,128)S(1)}, f32[4,4,16,256]{3,2,1,0:T(8,128)S(1)}, u32[]{:S(2)}, u32[]{:S(2)}) collective-permute-start(f32[4,4,16,256]{3,2,1,0:T(8,128)S(1)} %get-tuple-element.84), channel_id=1, source_target_pairs={{0,1},{1,0},{2,3},{3,2},{4,5},{5,4},{6,7},{7,6},{8,9},{9,8},{10,11... | collective-permute-start | bytes 786440 | tf_op jit(solution)/shard_map/ppermute | solution.py:148
  9.8 10.7 %collective-permute-start.31 = (f32[4,4,16,256]{3,2,1,0:T(8,128)S(1)}, f32[4,4,16,256]{3,2,1,0:T(8,128)S(1)}, u32[]{:S(2)}, u32[]{:S(2)}) collective-permute-start(f32[4,4,16,256]{3,2,1,0:T(8,128)S(1)} %get-tuple-element.75), channel_id=1, source_target_pairs={{0,1},{1,0},{2,3},{3,2},{4,5},{5,4},{6,7},{7,6},{8,9},{9,8},{10,11... | collective-permute-start | bytes 786440 | tf_op jit(solution)/shard_map/ppermute | solution.py:148
  12.5 10.1 %collective-permute-start.17 = (f32[4,4,16,256]{3,2,1,0:T(8,128)S(1)}, f32[4,4,16,256]{3,2,1,0:T(8,128)S(1)}, u32[]{:S(2)}, u32[]{:S(2)}) collective-permute-start(f32[4,4,16,256]{3,2,1,0:T(8,128)S(1)} %get-tuple-element.66), channel_id=1, source_target_pairs={{0,1},{1,0},{2,3},{3,2},{4,5},{5,4},{6,7},{7,6},{8,9},{9,8},{10,11... | collective-permute-start | bytes 786440 | tf_op jit(solution)/shard_map/ppermute | solution.py:148
  15.6 7.1 %collective-permute-start = (f32[4,4,16,256]{3,2,1,0:T(8,128)S(1)}, f32[4,4,16,256]{3,2,1,0:T(8,128)S(1)}, u32[]{:S(2)}, u32[]{:S(2)}) collective-permute-start(f32[4,4,16,256]{3,2,1,0:T(8,128)S(1)} %get-tuple-element.57), channel_id=1, source_target_pairs={{0,1},{1,0},{2,3},{3,2},{4,5},{5,4},{6,7},{7,6},{8,9},{9,8},{10,11... | collective-permute-start | bytes 786440 | tf_op jit(solution)/shard_map/ppermute | solution.py:148
  17.3 7.5 %collective-permute-start.47 = (f32[4,16,256]{2,1,0:T(8,128)S(1)}, f32[4,16,256]{2,1,0:T(8,128)S(1)}, u32[]{:S(2)}, u32[]{:S(2)}) collective-permute-start(f32[4,16,256]{2,1,0:T(8,128)S(1)} %get-tuple-element.88), channel_id=1, source_target_pairs={{0,2},{1,3},{2,0},{3,1},{4,6},{5,7},{6,4},{7,5},{8,10},{9,11},{10,... | collective-permute-start | bytes 196616 | tf_op jit(solution)/shard_map/ppermute | solution.py:148
  20.4 8.9 %collective-permute-start.46 = (f32[4,16,256]{2,1,0:T(8,128)S(1)}, f32[4,16,256]{2,1,0:T(8,128)S(1)}, u32[]{:S(2)}, u32[]{:S(2)}) collective-permute-start(f32[4,16,256]{2,1,0:T(8,128)S(1)} %get-tuple-element.86), channel_id=1, source_target_pairs={{0,2},{1,3},{2,0},{3,1},{4,6},{5,7},{6,4},{7,5},{8,10},{9,11},{10,... | collective-permute-start | bytes 196616 | tf_op jit(solution)/shard_map/ppermute | solution.py:148
  20.5 7.2 %collective-permute-start.33 = (f32[4,16,256]{2,1,0:T(8,128)S(1)}, f32[4,16,256]{2,1,0:T(8,128)S(1)}, u32[]{:S(2)}, u32[]{:S(2)}) collective-permute-start(f32[4,16,256]{2,1,0:T(8,128)S(1)} %get-tuple-element.79), channel_id=1, source_target_pairs={{0,2},{1,3},{2,0},{3,1},{4,6},{5,7},{6,4},{7,5},{8,10},{9,11},{10,... | collective-permute-start | bytes 196616 | tf_op jit(solution)/shard_map/ppermute | solution.py:148
  22.6 8.3 %collective-permute-start.19 = (f32[4,16,256]{2,1,0:T(8,128)S(1)}, f32[4,16,256]{2,1,0:T(8,128)S(1)}, u32[]{:S(2)}, u32[]{:S(2)}) collective-permute-start(f32[4,16,256]{2,1,0:T(8,128)S(1)} %get-tuple-element.70), channel_id=1, source_target_pairs={{0,2},{1,3},{2,0},{3,1},{4,6},{5,7},{6,4},{7,5},{8,10},{9,11},{10,... | collective-permute-start | bytes 196616 | tf_op jit(solution)/shard_map/ppermute | solution.py:148
  22.7 8.6 %collective-permute-start.2 = (f32[4,16,256]{2,1,0:T(8,128)S(1)}, f32[4,16,256]{2,1,0:T(8,128)S(1)}, u32[]{:S(2)}, u32[]{:S(2)}) collective-permute-start(f32[4,16,256]{2,1,0:T(8,128)S(1)} %get-tuple-element.61), channel_id=1, source_target_pairs={{0,2},{1,3},{2,0},{3,1},{4,6},{5,7},{6,4},{7,5},{8,10},{9,11},{10,... | collective-permute-start | bytes 196616 | tf_op jit(solution)/shard_map/ppermute | solution.py:148
  24.8 7.2 %collective-permute-start.48 = (f32[4,16,256]{2,1,0:T(8,128)S(1)}, f32[4,16,256]{2,1,0:T(8,128)S(1)}, u32[]{:S(2)}, u32[]{:S(2)}) collective-permute-start(f32[4,16,256]{2,1,0:T(8,128)S(1)} %add.29), channel_id=1, source_target_pairs={{0,4},{1,5},{2,6},{3,7},{4,0},{5,1},{6,2},{7,3},{8,12},{9,13},{10,... | collective-permute-start | bytes 196616 | tf_op jit(solution)/shard_map/ppermute | solution.py:148
  27.7 7.6 %collective-permute-start.7 = (f32[2,16,1024]{2,1,0:T(8,128)S(1)}, f32[2,16,1024]{2,1,0:T(8,128)S(1)}, u32[]{:S(2)}, u32[]{:S(2)}) collective-permute-start(f32[2,16,1024]{2,1,0:T(8,128)S(1)} %pad_maximum_fusion.refs_4_), channel_id=1, source_target_pairs={{0,8},{8,0},{16,24},{24,16},{1,9},{9,1},{17,25},{25,17},{2,10},{10... | collective-permute-start | bytes 393224 | tf_op jit(solution)/shard_map/ppermute | solution.py:148
  31.3 7.0 %collective-permute-start.32 = (f32[4,16,256]{2,1,0:T(8,128)S(1)}, f32[4,16,256]{2,1,0:T(8,128)S(1)}, u32[]{:S(2)}, u32[]{:S(2)}) collective-permute-start(f32[4,16,256]{2,1,0:T(8,128)S(1)} %get-tuple-element.77), channel_id=1, source_target_pairs={{0,2},{1,3},{2,0},{3,1},{4,6},{5,7},{6,4},{7,5},{8,10},{9,11},{10,... | collective-permute-start | bytes 196616 | tf_op jit(solution)/shard_map/ppermute | solution.py:148
  32.0 8.4 %collective-permute-start.34 = (f32[4,16,256]{2,1,0:T(8,128)S(1)}, f32[4,16,256]{2,1,0:T(8,128)S(1)}, u32[]{:S(2)}, u32[]{:S(2)}) collective-permute-start(f32[4,16,256]{2,1,0:T(8,128)S(1)} %add.28), channel_id=1, source_target_pairs={{0,4},{1,5},{2,6},{3,7},{4,0},{5,1},{6,2},{7,3},{8,12},{9,13},{10,... | collective-permute-start | bytes 196616 | tf_op jit(solution)/shard_map/ppermute | solution.py:148
  35.3 7.6 %collective-permute-start.18 = (f32[4,16,256]{2,1,0:T(8,128)S(1)}, f32[4,16,256]{2,1,0:T(8,128)S(1)}, u32[]{:S(2)}, u32[]{:S(2)}) collective-permute-start(f32[4,16,256]{2,1,0:T(8,128)S(1)} %get-tuple-element.68), channel_id=1, source_target_pairs={{0,2},{1,3},{2,0},{3,1},{4,6},{5,7},{6,4},{7,5},{8,10},{9,11},{10,... | collective-permute-start | bytes 196616 | tf_op jit(solution)/shard_map/ppermute | solution.py:148
  35.5 9.0 %collective-permute-start.1 = (f32[4,16,256]{2,1,0:T(8,128)S(1)}, f32[4,16,256]{2,1,0:T(8,128)S(1)}, u32[]{:S(2)}, u32[]{:S(2)}) collective-permute-start(f32[4,16,256]{2,1,0:T(8,128)S(1)} %get-tuple-element.59), channel_id=1, source_target_pairs={{0,2},{1,3},{2,0},{3,1},{4,6},{5,7},{6,4},{7,5},{8,10},{9,11},{10,... | collective-permute-start | bytes 196616 | tf_op jit(solution)/shard_map/ppermute | solution.py:148
  37.4 7.8 %collective-permute-start.20 = (f32[4,16,256]{2,1,0:T(8,128)S(1)}, f32[4,16,256]{2,1,0:T(8,128)S(1)}, u32[]{:S(2)}, u32[]{:S(2)}) collective-permute-start(f32[4,16,256]{2,1,0:T(8,128)S(1)} %add.27), channel_id=1, source_target_pairs={{0,4},{1,5},{2,6},{3,7},{4,0},{5,1},{6,2},{7,3},{8,12},{9,13},{10,... | collective-permute-start | bytes 196616 | tf_op jit(solution)/shard_map/ppermute | solution.py:148
  38.4 8.1 %collective-permute-start.3 = (f32[4,16,256]{2,1,0:T(8,128)S(1)}, f32[4,16,256]{2,1,0:T(8,128)S(1)}, u32[]{:S(2)}, u32[]{:S(2)}) collective-permute-start(f32[4,16,256]{2,1,0:T(8,128)S(1)} %add.26), channel_id=1, source_target_pairs={{0,4},{1,5},{2,6},{3,7},{4,0},{5,1},{6,2},{7,3},{8,12},{9,13},{10,... | collective-permute-start | bytes 196616 | tf_op jit(solution)/shard_map/ppermute | solution.py:148
  40.3 7.6 %collective-permute-start.49 = (f32[4,16,256]{2,1,0:T(8,128)S(1)}, f32[4,16,256]{2,1,0:T(8,128)S(1)}, u32[]{:S(2)}, u32[]{:S(2)}) collective-permute-start(f32[4,16,256]{2,1,0:T(8,128)S(1)} %momentum_0.1.refs_0_.refs_9_), channel_id=1, source_target_pairs={{0,8},{8,0},{16,24},{24,16},{1,9},{9,1},{17,25},{25,17},{2,10},{10... | collective-permute-start | bytes 196616 | tf_op jit(solution)/shard_map/ppermute | solution.py:148
  45.2 7.2 %collective-permute-start.35 = (f32[4,16,256]{2,1,0:T(8,128)S(1)}, f32[4,16,256]{2,1,0:T(8,128)S(1)}, u32[]{:S(2)}, u32[]{:S(2)}) collective-permute-start(f32[4,16,256]{2,1,0:T(8,128)S(1)} %momentum_1.1.refs_0_.refs_9_), channel_id=1, source_target_pairs={{0,8},{8,0},{16,24},{24,16},{1,9},{9,1},{17,25},{25,17},{2,10},{10... | collective-permute-start | bytes 196616 | tf_op jit(solution)/shard_map/ppermute | solution.py:148
  49.6 7.1 %collective-permute-start.21 = (f32[4,16,256]{2,1,0:T(8,128)S(1)}, f32[4,16,256]{2,1,0:T(8,128)S(1)}, u32[]{:S(2)}, u32[]{:S(2)}) collective-permute-start(f32[4,16,256]{2,1,0:T(8,128)S(1)} %momentum_2.1.refs_0_.refs_9_), channel_id=1, source_target_pairs={{0,8},{8,0},{16,24},{24,16},{1,9},{9,1},{17,25},{25,17},{2,10},{10... | collective-permute-start | bytes 196616 | tf_op jit(solution)/shard_map/ppermute | solution.py:148
  53.1 7.2 %collective-permute-start.4 = (f32[4,16,256]{2,1,0:T(8,128)S(1)}, f32[4,16,256]{2,1,0:T(8,128)S(1)}, u32[]{:S(2)}, u32[]{:S(2)}) collective-permute-start(f32[4,16,256]{2,1,0:T(8,128)S(1)} %momentum_3.1.refs_0_.refs_9_), channel_id=1, source_target_pairs={{0,8},{8,0},{16,24},{24,16},{1,9},{9,1},{17,25},{25,17},{2,10},{10... | collective-permute-start | bytes 196616 | tf_op jit(solution)/shard_map/ppermute | solution.py:148
  61.0 7.4 %collective-permute-start.41 = (f32[4,16,256]{2,1,0:T(8,128)S(1)}, f32[4,16,256]{2,1,0:T(8,128)S(1)}, u32[]{:S(2)}, u32[]{:S(2)}) collective-permute-start(f32[4,16,256]{2,1,0:T(8,128)S(1)} %get-tuple-element.80.refs_1_), channel_id=1, source_target_pairs={{0,4},{1,5},{2,6},{3,7},{4,0},{5,1},{6,2},{7,3},{8,12},{9,13},{10,... | collective-permute-start | bytes 196616 | tf_op jit(solution)/shard_map/ppermute | solution.py:148
  63.8 7.9 %collective-permute-start.27 = (f32[4,16,256]{2,1,0:T(8,128)S(1)}, f32[4,16,256]{2,1,0:T(8,128)S(1)}, u32[]{:S(2)}, u32[]{:S(2)}) collective-permute-start(f32[4,16,256]{2,1,0:T(8,128)S(1)} %get-tuple-element.71.refs_1_), channel_id=1, source_target_pairs={{0,4},{1,5},{2,6},{3,7},{4,0},{5,1},{6,2},{7,3},{8,12},{9,13},{10,... | collective-permute-start | bytes 196616 | tf_op jit(solution)/shard_map/ppermute | solution.py:148
  81.7 7.6 %collective-permute-start.10 = (f32[4,16,256]{2,1,0:T(8,128)S(1)}, f32[4,16,256]{2,1,0:T(8,128)S(1)}, u32[]{:S(2)}, u32[]{:S(2)}) collective-permute-start(f32[4,16,256]{2,1,0:T(8,128)S(1)} %get-tuple-element.62.refs_1_), channel_id=1, source_target_pairs={{0,1},{1,0},{2,3},{3,2},{4,5},{5,4},{6,7},{7,6},{8,9},{9,8},{10,11... | collective-permute-start | bytes 196616 | tf_op jit(solution)/shard_map/ppermute | solution.py:148
  (49 other events, 298.3 us)

commit v2 on v1

v2 whole, which is shorter than its diff:
```python
import functools

import jax
import jax.numpy as jnp
from jax import lax
from jax.experimental import pallas as pl
from jax.experimental.pallas import tpu as pltpu
from jax.sharding import PartitionSpec as P

LOCAL_RATE = 0.3
REGION_BETA = 0.9
REGION_RATE = 1.0
GLOBAL_MU = 0.9
GLOBAL_RATE = 0.7

CHUNKS = 2
F32 = jnp.float32
BF16 = jnp.bfloat16
VMEM = pl.BlockSpec(memory_space=pltpu.VMEM)
SMEM = pl.BlockSpec(memory_space=pltpu.SMEM)
HBM = pl.BlockSpec(memory_space=pltpu.HBM)


def call(kernel, out, in_specs, out_specs, moved, flops=0, grant=20, **kwargs):
    return pl.pallas_call(
        kernel,
        out_shape=out,
        in_specs=in_specs,
        out_specs=out_specs,
        cost_estimate=pl.CostEstimate(flops=flops, bytes_accessed=moved, transcendentals=0),
        compiler_params=pltpu.CompilerParams(vmem_limit_bytes=grant * 1024 * 1024),
        **kwargs,
    )


def exchange(value, axis, bits):
    size = lax.axis_size(axis)
    return lax.ppermute(value, axis, [(i, i ^ bits) for i in range(size)])


def place_of_mine():
    worker = lax.axis_index("worker")
    return lax.rem(worker, 2), lax.div(worker, 2)


def take_steps(x_ref, start, half_teacher, keep_ref, send_ref):
    core, chip = place_of_mine()
    chips, strips, rows, width = keep_ref.shape
    local_steps, tokens, _ = x_ref.shape
    scale = LOCAL_RATE / tokens

    def target(step):
        half = jnp.dot(x_ref[step], half_teacher, preferred_element_type=F32)
        return half + half * jnp.tanh(half)

    current = start
    wanted = target(0)
    for step in range(local_steps):
        x = x_ref[step]
        predicted = jnp.dot(x, current.astype(BF16), preferred_element_type=F32)
        residual = (predicted - wanted).astype(BF16)
        if step + 1 < local_steps:
            wanted = target(step + 1)
        gradient = lax.dot_general(
            x, residual, (((0,), (0,)), ((), ())), preferred_element_type=F32
        )
        current = current - scale * gradient
    pseudo = start - current
    for k in range(chips):
        slot = k ^ chip
        for s in range(strips):
            even = pseudo[2 * k * rows : (2 * k + 1) * rows, s * width : (s + 1) * width]
            odd = pseudo[(2 * k + 1) * rows : (2 * k + 2) * rows, s * width : (s + 1) * width]
            keep_ref[slot, s] = jnp.where(core == 0, even, odd)
            send_ref[slot, s] = jnp.where(core == 0, odd, even)


def halved(teacher):
    return (teacher.astype(F32) * 0.5).astype(BF16)


def first_kernel(stride, has_rest, x_hbm, w_hbm, t_hbm, keep_ref, send_ref, *refs):
    if has_rest:
        x_ref, w_rest, t_rest, w_ref, t_ref, sems = refs
    else:
        x_ref, w_ref, t_ref, sems = refs
    _, strips, _, width = keep_ref.shape
    now, later = [], []

    def copy(source, target, group):
        one = pltpu.make_async_copy(source, target, sems.at[len(now) + len(later)])
        one.start()
        group.append(one)

    copy(x_hbm, x_ref, now)
    for source, target in ((t_hbm, t_ref), (w_hbm, w_ref)):
        for s in range(strips):
            columns = pl.ds(s * width, width)
            copy(source.at[:, pl.ds(s * stride, width)], target.at[:, columns], now)
    if has_rest:
        for source, target in ((t_hbm, t_rest), (w_hbm, w_rest)):
            for s in range(strips):
                columns = pl.ds(s * stride + width, stride - width)
                copy(source.at[:, columns], target.at[s], later)
    for one in now:
        one.wait()
    take_steps(x_ref, w_ref[...].astype(F32), halved(t_ref[...]), keep_ref, send_ref)
    for one in later:
        one.wait()


def later_kernel(offset, x_ref, w_ref, t_ref, keep_ref, send_ref):
    _, strips, _, width = keep_ref.shape

    def columns(ref):
        return jnp.concatenate([ref[s, :, offset : offset + width] for s in range(strips)], 1)

    take_steps(x_ref, columns(w_ref).astype(F32), halved(columns(t_ref)), keep_ref, send_ref)


def add_kernel(keep_ref, got_ref, *out_refs):
    for k, out in enumerate(out_refs):
        out[...] = keep_ref[k] + got_ref[k]


def momentum_kernel(offset, stride, workers, *refs):
    *parts, old_ref, out_ref = refs
    strips, _, width = out_ref.shape
    for s in range(strips):
        total = parts[0][s]
        for part in parts[1:]:
            total = total + part[s]
        first = s * stride + offset
        out_ref[s] = REGION_RATE * (
            REGION_BETA * old_ref[:, first : first + width] + total / workers
        )


def coefficient_kernel(stale_ref, arrival_ref, slot_ref, coef_ref):
    _, regions, width = coef_ref.shape
    regions -= 1
    step, own, carried = [], [], []
    total, power = 1.0, 1.0
    for _ in range(regions):
        carried.append(power)
        power *= GLOBAL_MU
        total += power
        step.append(GLOBAL_RATE * total)
        own.append(GLOBAL_RATE * GLOBAL_MU * (total - 1.0))

    def pick(table, index):
        value = jnp.zeros((1, width), F32)
        for i, entry in enumerate(table):
            value = jnp.where(index == i, entry, value)
        return value

    region = lax.axis_index("region")
    slot, last = slot_ref[region], regions - 1
    for q in range(regions):
        other = region ^ q
        position = jnp.int32(0)
        for k in range(regions):
            position = jnp.where(arrival_ref[k] == other, k, position)
        weight = 1.0 / (1.0 + jnp.full((1, width), stale_ref[other], jnp.int32).astype(F32))
        coef_ref[0, q : q + 1] = weight * pick(step, slot - position)
        coef_ref[1, q : q + 1] = weight * pick(step, last - position)
        coef_ref[2, q : q + 1] = weight * pick(carried, last - position)
    coef_ref[0, regions : regions + 1] = pick(own, slot)
    coef_ref[1, regions : regions + 1] = jnp.full((1, width), own[last], F32)
    coef_ref[2, regions : regions + 1] = jnp.full((1, width), power, F32)


def merge_kernel(offset, regions, coef_ref, *refs):
    deltas, states = refs[:regions], refs[regions : 2 * regions]
    pulled_ref, params_ref, momentum_ref = refs[2 * regions :]
    me = lax.axis_index("region")
    width = pulled_ref.shape[2]

    def coef(row, column):
        return coef_ref[row, column : column + 1]

    for q in range(regions):
        strip = me ^ q
        params = states[q][0, :, offset : offset + width]
        momentum = states[q][1, :, offset : offset + width]
        terms = [deltas[p][strip] for p in range(regions)]
        pulled = params - coef(0, regions) * momentum
        for p in range(regions):
            pulled = pulled - coef(0, p) * terms[p]
        pulled_ref[strip] = pulled
        if q == 0:
            last = params - coef(1, regions) * momentum
            carried = coef(2, regions) * momentum
            for p in range(regions):
                last = last - coef(1, p) * terms[p]
                carried = carried + coef(2, p) * terms[p]
            params_ref[...] = last
            momentum_ref[...] = carried


def place_kernel(offset, stride, owners, side, aliased, *refs):
    count = len(owners) + (3 if side else 0)
    parts, outs, sems = refs[:count], refs[count + aliased : -1], refs[-1]
    core, chip = place_of_mine()
    strips, _, width = parts[0].shape
    copies = []

    def copy(source, target):
        copies.append(pltpu.make_async_copy(source, target, sems.at[len(copies)]))
        copies[-1].start()

    for s in range(strips):
        columns = pl.ds(s * stride + offset, width)
        for part, b in zip(parts, owners):
            owner = 2 * (chip ^ (b // 2)) + (core ^ (b % 2))
            copy(part.at[s], outs[0].at[owner, :, columns])
        if side:
            copy(parts[-3].at[s], outs[1].at[:, columns])
    if side:
        copy(parts[-2], outs[2].at[:, pl.ds(offset, width)])
        copy(parts[-1], outs[3].at[:, pl.ds(offset, width)])
    for one in copies:
        one.wait()


def scatter_sum(blocks):
    bit, count = 1, len(blocks)
    while count > 4:
        got = exchange(jnp.stack(blocks[1::2]), "worker", 2 * bit)
        blocks = [b + got[i] for i, b in enumerate(blocks[0::2])]
        bit, count = 2 * bit, count // 2
    if count == 4:
        far = exchange(blocks[3], "worker", 2 * bit)
        near = exchange(blocks[1], "worker", 2 * bit)
        across = exchange(blocks[2] + far, "worker", 4 * bit)
        return [blocks[0], near, across]
    if count == 2:
        return [blocks[0], exchange(blocks[1], "worker", 2 * bit)]
    return blocks


def gather_blocks(block, chips):
    levels = chips.bit_length() - 1
    if levels >= 2:
        bit = chips // 4
        across = exchange(block, "worker", 4 * bit)
        near = exchange(block, "worker", 2 * bit)
        far = exchange(across, "worker", 2 * bit)
        blocks, bit = [block, near, across, far], bit // 2
    elif levels == 1:
        blocks, bit = [block, exchange(block, "worker", 2)], 0
    else:
        blocks, bit = [block], 0
    while bit >= 1:
        got = exchange(jnp.stack(blocks), "worker", 2 * bit)
        blocks = [part for i, b in enumerate(blocks) for part in (b, got[i])]
        bit //= 2
    return [part for b in blocks for part in (b, exchange(b, "worker", 1))]


def local(
    worker_start,
    inputs,
    teacher,
    regional_momentum,
    global_params,
    global_momentum,
    staleness,
    arrival_order,
    pull_slot,
):
    initial, hidden, old = worker_start[0], inputs[0, 0], regional_momentum[0]
    depth, wide = initial.shape
    workers, regions = lax.axis_size("worker"), lax.axis_size("region")
    chips, rows, stride = workers // 2, depth // workers, wide // regions
    chunks = min(CHUNKS, stride // 128)
    width = stride // chunks

    def shape(*dims, dtype=F32):
        return jax.ShapeDtypeStruct(dims, dtype)

    coef = call(
        coefficient_kernel, shape(3, regions + 1, width), [SMEM] * 3, VMEM, 4096
    )(staleness, arrival_order, pull_slot)
    state = jnp.stack([global_params, global_momentum])
    states = [state] + [exchange(state, "region", q) for q in range(1, regions)]

    block = shape(regions, rows, width)
    half = shape(chips, regions, rows, width)
    block_bytes = regions * rows * width * 4
    flops = 6 * hidden.shape[0] * hidden.shape[1] * depth * width * regions
    has_rest = chunks > 1
    rest = (shape(regions, depth, stride - width, dtype=initial.dtype),) * 2 if has_rest else ()
    chunk_columns = pltpu.VMEM((depth, regions * width), initial.dtype)
    keep, send, x_ready, *ready = call(
        functools.partial(first_kernel, stride, has_rest),
        (half, half, shape(*hidden.shape, dtype=hidden.dtype), *rest),
        [HBM] * 3,
        (VMEM,) * (3 + len(rest)),
        2 * workers * block_bytes,
        flops,
        grant=51,
        scratch_shapes=[
            chunk_columns, chunk_columns, pltpu.SemaphoreType.DMA((1 + 4 * regions,))
        ],
    )(hidden, initial, teacher)
    halves = [(keep, send)]
    for j in range(1, chunks):
        halves.append(
            call(
                functools.partial(later_kernel, (j - 1) * width),
                (half, half), [VMEM] * 3, (VMEM,) * 2, 2 * workers * block_bytes, flops,
            )(x_ready, ready[0], ready[1])
        )
    outs = ()
    shapes = (
        shape(workers, rows, wide), shape(rows, wide), shape(rows, stride), shape(rows, stride)
    )
    for j, (keep, send) in enumerate(halves):
        offset = j * width
        got = exchange(send, "worker", 1)
        blocks = call(
            add_kernel, (block,) * chips, [VMEM] * 2, (VMEM,) * chips,
            3 * chips * block_bytes,
        )(keep, got)
        parts = scatter_sum(blocks)
        delta = call(
            functools.partial(momentum_kernel, offset, stride, workers),
            block, [VMEM] * (len(parts) + 1), VMEM, (len(parts) + 2) * block_bytes,
        )(*parts, old)
        deltas = [delta]
        for q in range(1, regions):
            deltas.append(exchange(delta, "region", q))
        pulled, last, carried = call(
            functools.partial(merge_kernel, offset, regions),
            (block, shape(rows, width), shape(rows, width)),
            [VMEM] * (2 * regions + 1), (VMEM,) * 3, (regions + 4) * block_bytes,
        )(coef, *deltas, *states)
        pieces = gather_blocks(pulled, chips)
        early = [0, 1, 2, 4] if chips == 4 else list(range(workers // 2))
        late = [b for b in range(workers) if b not in early]
        for part, owners in (("a", early), ("b", late)):
            side = part == "a"
            given = [pieces[b] for b in owners] + ([delta, last, carried] if side else [])
            outs = call(
                functools.partial(place_kernel, offset, stride, owners, side, len(outs)),
                shapes,
                [VMEM] * len(given) + [HBM] * len(outs),
                (HBM,) * 4,
                2 * len(given) * block_bytes,
                scratch_shapes=[pltpu.SemaphoreType.DMA((regions * (len(owners) + 1) + 2,))],
                input_output_aliases={len(given) + i: i for i in range(len(outs))},
            )(*given, *outs)
    pulled, regional, params, momentum = outs
    return (regional[None], params, momentum, pulled.reshape(depth, wide)[None])


def solution(mesh):
    placed = (
        P("region", None, None),
        P("region", "worker", None, None, None),
        P(),
        P("region", "worker", None),
        P("worker", "region"),
        P("worker", "region"),
        P(),
        P(),
        P(),
    )

    return jax.shard_map(
        local,
        mesh=mesh,
        in_specs=placed,
        out_specs=(
            P("region", "worker", None),
            P("worker", "region"),
            P("worker", "region"),
            P("region", None, None),
        ),
        check_vma=False,
    )
```

time: 91.3 us -> 66 us (0.72)
  starting transfers between devices: 51.7 us -> 32.5 us
  waiting for transfers between devices: 11.3 us -> 18.4 us
  Pallas kernels: 19.6 us -> 13 us
  other arithmetic: 3.87 us -> 0.05 us
  local copies, waits for them, and re-layouts: 3.56 us -> 0.98 us
    ppermute x59 -> x31, starting transfers between devices: 51.7 us -> 32.5 us  [exchange(): return lax.ppermute(value, axis, [(i, i ^ bits) for i in range(size)])]
    ppermute x59 -> x31, waiting for transfers between devices: 11.3 us -> 18.4 us  [exchange(): return lax.ppermute(value, axis, [(i, i ^ bits) for i in range(size)])]
    pallas_call x16 -> x11, Pallas kernels: 19.5 us -> 12.9 us  [the longest x1 4.74 us: local(): call(functools.partial(first_kernel, stride, has_rest), (half, half, shap...]
    unnamed x28 -> x14, local copies, waits for them, and re-layouts: 3.47 us -> 0.98 us
    reduce_sum x4 -> x0, other arithmetic: 2.27 us -> none  [the longest x2 1.46 us: pick(): return jnp.sum(jnp.where(hit, jnp.array(table, F32), 0.0), axis=-1)]
  transfers between devices with their start and end apart: 59 -> 31, of which waited for: 7 -> 14; matrix products, arithmetic and copies ran while one was open for 4% -> 0% of each run, Pallas kernels for 17% -> 11%
where the time goes in v2:
time: 66 us; the launch traced here: 65.8 us
  starting transfers between devices  32.5 us (49%)
  waiting for transfers between devices  18.4 us (28%)
  Pallas kernels  13 us (20%)
  local copies, waits for them, and re-layouts  0.98 us (1%)
  between operations  0.87 us (1%)
    ppermute x31, starting transfers between devices, exchange(): return lax.ppermute(value, axis, [(i, i ^ bits) for i in range(size)])  32.5 us
    ppermute x31, waiting for transfers between devices, exchange(): return lax.ppermute(value, axis, [(i, i ^ bits) for i in range(size)])  18.4 us
    pallas_call x1, Pallas kernels, local(): call(functools.partial(first_kernel, stride, has_rest), (half, half, shap...  4.74 us
    pallas_call x4, Pallas kernels, local(): call(functools.partial(place_kernel, offset, stride, owners, side, len(ou...  4.05 us
    pallas_call x1, Pallas kernels, local(): call(functools.partial(later_kernel, (j - 1) * width), (half, half), [VME...  3.25 us
  transfers between devices with their start and end apart: 31, of which 14 were waited for; matrix products, arithmetic and copies ran while one was open for 0% of the time, Pallas kernels for 11%

profile of v2, /device:TPU:0, one launch (start us, length us, event | category | flops | bytes accessed | tf_op | source)
XLA Modules:
  0.0 65.8 jit_solution(10922376632143377730)
XLA Ops:
  1.6 4.7 %shard_map.121 = (f32[4,4,16,512]{3,2,1,0:T(8,128)S(1)}, f32[4,4,16,512]{3,2,1,0:T(8,128)S(1)}, bf16[4,256,128]{2,1,0:T(8,128)(2,1)S(1)}, bf16[4,128,512]{2,1,0:T(8,128)(2,1)S(1)}, bf16[4,128,512]{2,1,0:T(8,128)(2,1)S(1)}) custom-call(bf16[4,256,128]{2,1,0:T(8,128)(2,1)S(1)} %bitcast.9, bf16[128,4096]{1,0:T(8,128)(2,1)} %bitcast.14, bf16[128,4096]{1,0:T(8,128)(2,1)} %t_hbm.1), custom_call_target="tpu_custom_call" | custom-call | flops 1610612736 | bytes 2097152 | tf_op jit(solution)/shard_map/pallas_call | solution.py:295
  6.9 3.3 %shard_map.122 = (f32[4,4,16,512]{3,2,1,0:T(8,128)S(1)}, f32[4,4,16,512]{3,2,1,0:T(8,128)S(1)}) custom-call(bf16[4,256,128]{2,1,0:T(8,128)(2,1)S(1)} %get-tuple-element.41.x_ref, bf16[4,128,512]{2,1,0:T(8,128)(2,1)S(1)} %get-tuple-element.42.w_ref, bf16[4,128,512]{2,1,0:T(8,128)(2,1)S(1)} %get-tuple-element.43.t_ref), custom_call_target="tpu_custom_call" | custom-call | flops 1610612736 | bytes 2097152 | tf_op jit(solution)/shard_map/pallas_call | solution.py:310
  10.4 3.1 %collective-permute-start.19 = (f32[4,16,512]{2,1,0:T(8,128)S(1)}, f32[4,16,512]{2,1,0:T(8,128)S(1)}, u32[]{:S(2)}, u32[]{:S(2)}) collective-permute-start(f32[4,16,512]{2,1,0:T(8,128)S(1)} %get-tuple-element.58), channel_id=1, source_target_pairs={{0,2},{1,3},{2,0},{3,1},{4,6},{5,7},{6,4},{7,5},{8,10},{9,11},{10,... | collective-permute-start | bytes 393224 | tf_op jit(solution)/shard_map/ppermute | solution.py:38
  13.6 1.4 %collective-permute-start.2 = (f32[4,16,512]{2,1,0:T(8,128)S(1)}, f32[4,16,512]{2,1,0:T(8,128)S(1)}, u32[]{:S(2)}, u32[]{:S(2)}) collective-permute-start(f32[4,16,512]{2,1,0:T(8,128)S(1)} %get-tuple-element.49), channel_id=1, source_target_pairs={{0,2},{1,3},{2,0},{3,1},{4,6},{5,7},{6,4},{7,5},{8,10},{9,11},{10,... | collective-permute-start | bytes 393224 | tf_op jit(solution)/shard_map/ppermute | solution.py:38
  15.6 2.2 %collective-permute-done.19 = f32[4,16,512]{2,1,0:T(8,128)S(1)} collective-permute-done((f32[4,16,512]{2,1,0:T(8,128)S(1)}, f32[4,16,512]{2,1,0:T(8,128)S(1)}, u32[]{:S(2)}, u32[]{:S(2)}) %collective-permute-start.19) | collective-permute-done | bytes 131104 | tf_op jit(solution)/shard_map/ppermute | solution.py:38
  17.9 3.1 %collective-permute-start.20 = (f32[4,16,512]{2,1,0:T(8,128)S(1)}, f32[4,16,512]{2,1,0:T(8,128)S(1)}, u32[]{:S(2)}, u32[]{:S(2)}) collective-permute-start(f32[4,16,512]{2,1,0:T(8,128)S(1)} %add.7), channel_id=1, source_target_pairs={{0,4},{1,5},{2,6},{3,7},{4,0},{5,1},{6,2},{7,3},{8,12},{9,13},{10,... | collective-permute-start | bytes 393224 | tf_op jit(solution)/shard_map/ppermute | solution.py:38
  21.0 2.5 %collective-permute-start.9 = (f32[2,16,1024]{2,1,0:T(8,128)S(1)}, f32[2,16,1024]{2,1,0:T(8,128)S(1)}, u32[]{:S(2)}, u32[]{:S(2)}) collective-permute-start(f32[2,16,1024]{2,1,0:T(8,128)S(1)} %pad_maximum_fusion.refs_4_), channel_id=1, source_target_pairs={{0,24},{8,16},{16,8},{24,0},{1,25},{9,17},{17,9},{25,1},{2,26},{10... | collective-permute-start | bytes 393224 | tf_op jit(solution)/shard_map/ppermute | solution.py:38
  23.5 1.6 %collective-permute-start.1 = (f32[4,16,512]{2,1,0:T(8,128)S(1)}, f32[4,16,512]{2,1,0:T(8,128)S(1)}, u32[]{:S(2)}, u32[]{:S(2)}) collective-permute-start(f32[4,16,512]{2,1,0:T(8,128)S(1)} %get-tuple-element.47), channel_id=1, source_target_pairs={{0,2},{1,3},{2,0},{3,1},{4,6},{5,7},{6,4},{7,5},{8,10},{9,11},{10,... | collective-permute-start | bytes 393224 | tf_op jit(solution)/shard_map/ppermute | solution.py:38
  26.3 2.7 %collective-permute-start.8 = (f32[2,16,1024]{2,1,0:T(8,128)S(1)}, f32[2,16,1024]{2,1,0:T(8,128)S(1)}, u32[]{:S(2)}, u32[]{:S(2)}) collective-permute-start(f32[2,16,1024]{2,1,0:T(8,128)S(1)} %pad_maximum_fusion.refs_4_), channel_id=1, source_target_pairs={{0,16},{8,24},{16,0},{24,8},{1,17},{9,25},{17,1},{25,9},{2,18},{10... | collective-permute-start | bytes 393224 | tf_op jit(solution)/shard_map/ppermute | solution.py:38
  29.0 2.0 %collective-permute-start.7 = (f32[2,16,1024]{2,1,0:T(8,128)S(1)}, f32[2,16,1024]{2,1,0:T(8,128)S(1)}, u32[]{:S(2)}, u32[]{:S(2)}) collective-permute-start(f32[2,16,1024]{2,1,0:T(8,128)S(1)} %pad_maximum_fusion.refs_4_), channel_id=1, source_target_pairs={{0,8},{8,0},{16,24},{24,16},{1,9},{9,1},{17,25},{25,17},{2,10},{10... | collective-permute-start | bytes 393224 | tf_op jit(solution)/shard_map/ppermute | solution.py:38
  31.1 1.8 %collective-permute-start.22 = (f32[4,16,512]{2,1,0:T(8,128)S(1)}, f32[4,16,512]{2,1,0:T(8,128)S(1)}, u32[]{:S(2)}, u32[]{:S(2)}) collective-permute-start(f32[4,16,512]{2,1,0:T(8,128)S(1)} %shard_map.127.refs_0_.refs_4_), channel_id=1, source_target_pairs={{0,16},{8,24},{16,0},{24,8},{1,17},{9,25},{17,1},{25,9},{2,18},{10... | collective-permute-start | bytes 393224 | tf_op jit(solution)/shard_map/ppermute | solution.py:38
  34.7 1.2 %collective-permute-start.6 = (f32[4,16,512]{2,1,0:T(8,128)S(1)}, f32[4,16,512]{2,1,0:T(8,128)S(1)}, u32[]{:S(2)}, u32[]{:S(2)}) collective-permute-start(f32[4,16,512]{2,1,0:T(8,128)S(1)} %shard_map.124.refs_0_.refs_4_), channel_id=1, source_target_pairs={{0,24},{8,16},{16,8},{24,0},{1,25},{9,17},{17,9},{25,1},{2,26},{10... | collective-permute-start | bytes 393224 | tf_op jit(solution)/shard_map/ppermute | solution.py:38
  35.8 1.6 %collective-permute-start.5 = (f32[4,16,512]{2,1,0:T(8,128)S(1)}, f32[4,16,512]{2,1,0:T(8,128)S(1)}, u32[]{:S(2)}, u32[]{:S(2)}) collective-permute-start(f32[4,16,512]{2,1,0:T(8,128)S(1)} %shard_map.124.refs_0_.refs_4_), channel_id=1, source_target_pairs={{0,16},{8,24},{16,0},{24,8},{1,17},{9,25},{17,1},{25,9},{2,18},{10... | collective-permute-start | bytes 393224 | tf_op jit(solution)/shard_map/ppermute | solution.py:38
  41.0 1.7 %collective-permute-done.6.refs_3_ = f32[4,16,512]{2,1,0:T(8,128)S(1)} collective-permute-done((f32[4,16,512]{2,1,0:T(8,128)S(1)}, f32[4,16,512]{2,1,0:T(8,128)S(1)}, u32[]{:S(2)}, u32[]{:S(2)}) %collective-permute-start.6) | collective-permute-done | bytes 131104 | tf_op jit(solution)/shard_map/ppermute | solution.py:38
  44.0 1.3 %collective-permute-start.12 = (f32[4,16,512]{2,1,0:T(8,128)S(1)}, f32[4,16,512]{2,1,0:T(8,128)S(1)}, u32[]{:S(2)}, u32[]{:S(2)}) collective-permute-start(f32[4,16,512]{2,1,0:T(8,128)S(1)} %get-tuple-element.50.refs_0_), channel_id=1, source_target_pairs={{0,4},{1,5},{2,6},{3,7},{4,0},{5,1},{6,2},{7,3},{8,12},{9,13},{10,... | collective-permute-start | bytes 393224 | tf_op jit(solution)/shard_map/ppermute | solution.py:38
  45.3 3.1 %collective-permute-start.10 = (f32[4,16,512]{2,1,0:T(8,128)S(1)}, f32[4,16,512]{2,1,0:T(8,128)S(1)}, u32[]{:S(2)}, u32[]{:S(2)}) collective-permute-start(f32[4,16,512]{2,1,0:T(8,128)S(1)} %get-tuple-element.50.refs_0_), channel_id=1, source_target_pairs={{0,2},{1,3},{2,0},{3,1},{4,6},{5,7},{6,4},{7,5},{8,10},{9,11},{10,... | collective-permute-start | bytes 393224 | tf_op jit(solution)/shard_map/ppermute | solution.py:38
  49.3 1.8 %collective-permute-start.28 = (f32[4,16,512]{2,1,0:T(8,128)S(1)}, f32[4,16,512]{2,1,0:T(8,128)S(1)}, u32[]{:S(2)}, u32[]{:S(2)}) collective-permute-start(f32[4,16,512]{2,1,0:T(8,128)S(1)} %collective-permute-done.26.refs_3_), channel_id=1, source_target_pairs={{0,2},{1,3},{2,0},{3,1},{4,6},{5,7},{6,4},{7,5},{8,10},{9,11},{10,... | collective-permute-start | bytes 393224 | tf_op jit(solution)/shard_map/ppermute | solution.py:38
  51.1 2.1 %collective-permute-done.12.refs_3_ = f32[4,16,512]{2,1,0:T(8,128)S(1)} collective-permute-done((f32[4,16,512]{2,1,0:T(8,128)S(1)}, f32[4,16,512]{2,1,0:T(8,128)S(1)}, u32[]{:S(2)}, u32[]{:S(2)}) %collective-permute-start.12) | collective-permute-done | bytes 131104 | tf_op jit(solution)/shard_map/ppermute | solution.py:38
  53.3 1.7 %collective-permute-done.10.refs_2_ = f32[4,16,512]{2,1,0:T(8,128)S(1)} collective-permute-done((f32[4,16,512]{2,1,0:T(8,128)S(1)}, f32[4,16,512]{2,1,0:T(8,128)S(1)}, u32[]{:S(2)}, u32[]{:S(2)}) %collective-permute-start.10) | collective-permute-done | bytes 131104 | tf_op jit(solution)/shard_map/ppermute | solution.py:38
  54.9 2.8 %collective-permute-done.24.refs_2_ = f32[4,16,512]{2,1,0:T(8,128)S(1)} collective-permute-done((f32[4,16,512]{2,1,0:T(8,128)S(1)}, f32[4,16,512]{2,1,0:T(8,128)S(1)}, u32[]{:S(2)}, u32[]{:S(2)}) %collective-permute-start.24) | collective-permute-done | bytes 131104 | tf_op jit(solution)/shard_map/ppermute | solution.py:38
  57.7 2.0 %collective-permute-done.28.refs_2_ = f32[4,16,512]{2,1,0:T(8,128)S(1)} collective-permute-done((f32[4,16,512]{2,1,0:T(8,128)S(1)}, f32[4,16,512]{2,1,0:T(8,128)S(1)}, u32[]{:S(2)}, u32[]{:S(2)}) %collective-permute-start.28) | collective-permute-done | bytes 131104 | tf_op jit(solution)/shard_map/ppermute | solution.py:38
  61.7 1.0 %shard_map.129 = (f32[8,16,4096]{2,1,0:T(8,128)}, f32[16,4096]{1,0:T(8,128)}, f32[16,1024]{1,0:T(8,128)}, f32[16,1024]{1,0:T(8,128)}) custom-call(f32[4,16,512]{2,1,0:T(8,128)S(1)} %get-tuple-element.59.refs_0_, f32[4,16,512]{2,1,0:T(8,128)S(1)} %collective-permute-done.30.refs_1_, f32[4,16,512]{2,1,0:T(8,128)S(1)} %collective-permute-done.24.refs_2_, ...), custom_call_target="tpu_custom_call" | custom-call | bytes 1835008 | tf_op jit(solution)/shard_map/pallas_call | solution.py:345
  63.7 1.0 %shard_map.131 = (f32[8,16,4096]{2,1,0:T(8,128)}, f32[16,4096]{1,0:T(8,128)}, f32[16,1024]{1,0:T(8,128)}, f32[16,1024]{1,0:T(8,128)}) custom-call(f32[4,16,512]{2,1,0:T(8,128)S(1)} %get-tuple-element.50.refs_0_, f32[4,16,512]{2,1,0:T(8,128)S(1)} %collective-permute-done.16.refs_1_, ...), custom_call_target="tpu_custom_call", output_to_operand_aliasing={{0}: (7, {}), {1}: (8, {}), {2}: (9, {}), {3}: (10, {})} | custom-call | bytes 1835008 | tf_op jit(solution)/shard_map/pallas_call | solution.py:345
  64.8 1.0 %shard_map.132 = (f32[8,16,4096]{2,1,0:T(8,128)}, f32[16,4096]{1,0:T(8,128)}, f32[16,1024]{1,0:T(8,128)}, f32[16,1024]{1,0:T(8,128)}) custom-call(f32[4,16,512]{2,1,0:T(8,128)S(1)} %collective-permute-done.11.refs_0_, f32[4,16,512]{2,1,0:T(8,128)S(1)} %collective-permute-done.13.refs_1_, ...), custom_call_target="tpu_custom_call", output_to_operand_aliasing={{0}: (4, {}), {1}: (5, {}), {2}: (6, {}), {3}: (7, {})} | custom-call | bytes 1048576 | tf_op jit(solution)/shard_map/pallas_call | solution.py:345
  (68 shorter events, 14.2 us)
Async XLA Ops:
  10.4 7.5 %collective-permute-start.19 = (f32[4,16,512]{2,1,0:T(8,128)S(1)}, f32[4,16,512]{2,1,0:T(8,128)S(1)}, u32[]{:S(2)}, u32[]{:S(2)}) collective-permute-start(f32[4,16,512]{2,1,0:T(8,128)S(1)} %get-tuple-element.58), channel_id=1, source_target_pairs={{0,2},{1,3},{2,0},{3,1},{4,6},{5,7},{6,4},{7,5},{8,10},{9,11},{10,... | collective-permute-start | bytes 393224 | tf_op jit(solution)/shard_map/ppermute | solution.py:38
  13.6 11.5 %collective-permute-start.2 = (f32[4,16,512]{2,1,0:T(8,128)S(1)}, f32[4,16,512]{2,1,0:T(8,128)S(1)}, u32[]{:S(2)}, u32[]{:S(2)}) collective-permute-start(f32[4,16,512]{2,1,0:T(8,128)S(1)} %get-tuple-element.49), channel_id=1, source_target_pairs={{0,2},{1,3},{2,0},{3,1},{4,6},{5,7},{6,4},{7,5},{8,10},{9,11},{10,... | collective-permute-start | bytes 393224 | tf_op jit(solution)/shard_map/ppermute | solution.py:38
  15.0 11.3 %collective-permute-start.18 = (f32[4,16,512]{2,1,0:T(8,128)S(1)}, f32[4,16,512]{2,1,0:T(8,128)S(1)}, u32[]{:S(2)}, u32[]{:S(2)}) collective-permute-start(f32[4,16,512]{2,1,0:T(8,128)S(1)} %get-tuple-element.56), channel_id=1, source_target_pairs={{0,2},{1,3},{2,0},{3,1},{4,6},{5,7},{6,4},{7,5},{8,10},{9,11},{10,... | collective-permute-start | bytes 393224 | tf_op jit(solution)/shard_map/ppermute | solution.py:38
  17.9 11.1 %collective-permute-start.20 = (f32[4,16,512]{2,1,0:T(8,128)S(1)}, f32[4,16,512]{2,1,0:T(8,128)S(1)}, u32[]{:S(2)}, u32[]{:S(2)}) collective-permute-start(f32[4,16,512]{2,1,0:T(8,128)S(1)} %add.7), channel_id=1, source_target_pairs={{0,4},{1,5},{2,6},{3,7},{4,0},{5,1},{6,2},{7,3},{8,12},{9,13},{10,... | collective-permute-start | bytes 393224 | tf_op jit(solution)/shard_map/ppermute | solution.py:38
  21.0 10.1 %collective-permute-start.9 = (f32[2,16,1024]{2,1,0:T(8,128)S(1)}, f32[2,16,1024]{2,1,0:T(8,128)S(1)}, u32[]{:S(2)}, u32[]{:S(2)}) collective-permute-start(f32[2,16,1024]{2,1,0:T(8,128)S(1)} %pad_maximum_fusion.refs_4_), channel_id=1, source_target_pairs={{0,24},{8,16},{16,8},{24,0},{1,25},{9,17},{17,9},{25,1},{2,26},{10... | collective-permute-start | bytes 393224 | tf_op jit(solution)/shard_map/ppermute | solution.py:38
  23.5 7.6 %collective-permute-start.1 = (f32[4,16,512]{2,1,0:T(8,128)S(1)}, f32[4,16,512]{2,1,0:T(8,128)S(1)}, u32[]{:S(2)}, u32[]{:S(2)}) collective-permute-start(f32[4,16,512]{2,1,0:T(8,128)S(1)} %get-tuple-element.47), channel_id=1, source_target_pairs={{0,2},{1,3},{2,0},{3,1},{4,6},{5,7},{6,4},{7,5},{8,10},{9,11},{10,... | collective-permute-start | bytes 393224 | tf_op jit(solution)/shard_map/ppermute | solution.py:38
  25.1 8.7 %collective-permute-start.3 = (f32[4,16,512]{2,1,0:T(8,128)S(1)}, f32[4,16,512]{2,1,0:T(8,128)S(1)}, u32[]{:S(2)}, u32[]{:S(2)}) collective-permute-start(f32[4,16,512]{2,1,0:T(8,128)S(1)} %add.6), channel_id=1, source_target_pairs={{0,4},{1,5},{2,6},{3,7},{4,0},{5,1},{6,2},{7,3},{8,12},{9,13},{10,... | collective-permute-start | bytes 393224 | tf_op jit(solution)/shard_map/ppermute | solution.py:38
  26.3 8.4 %collective-permute-start.8 = (f32[2,16,1024]{2,1,0:T(8,128)S(1)}, f32[2,16,1024]{2,1,0:T(8,128)S(1)}, u32[]{:S(2)}, u32[]{:S(2)}) collective-permute-start(f32[2,16,1024]{2,1,0:T(8,128)S(1)} %pad_maximum_fusion.refs_4_), channel_id=1, source_target_pairs={{0,16},{8,24},{16,0},{24,8},{1,17},{9,25},{17,1},{25,9},{2,18},{10... | collective-permute-start | bytes 393224 | tf_op jit(solution)/shard_map/ppermute | solution.py:38
  29.0 6.9 %collective-permute-start.7 = (f32[2,16,1024]{2,1,0:T(8,128)S(1)}, f32[2,16,1024]{2,1,0:T(8,128)S(1)}, u32[]{:S(2)}, u32[]{:S(2)}) collective-permute-start(f32[2,16,1024]{2,1,0:T(8,128)S(1)} %pad_maximum_fusion.refs_4_), channel_id=1, source_target_pairs={{0,8},{8,0},{16,24},{24,16},{1,9},{9,1},{17,25},{25,17},{2,10},{10... | collective-permute-start | bytes 393224 | tf_op jit(solution)/shard_map/ppermute | solution.py:38
  31.0 6.4 %collective-permute-start.23 = (f32[4,16,512]{2,1,0:T(8,128)S(1)}, f32[4,16,512]{2,1,0:T(8,128)S(1)}, u32[]{:S(2)}, u32[]{:S(2)}) collective-permute-start(f32[4,16,512]{2,1,0:T(8,128)S(1)} %shard_map.127.refs_0_.refs_4_), channel_id=1, source_target_pairs={{0,24},{8,16},{16,8},{24,0},{1,25},{9,17},{17,9},{25,1},{2,26},{10... | collective-permute-start | bytes 393224 | tf_op jit(solution)/shard_map/ppermute | solution.py:38
  31.1 8.3 %collective-permute-start.22 = (f32[4,16,512]{2,1,0:T(8,128)S(1)}, f32[4,16,512]{2,1,0:T(8,128)S(1)}, u32[]{:S(2)}, u32[]{:S(2)}) collective-permute-start(f32[4,16,512]{2,1,0:T(8,128)S(1)} %shard_map.127.refs_0_.refs_4_), channel_id=1, source_target_pairs={{0,16},{8,24},{16,0},{24,8},{1,17},{9,25},{17,1},{25,9},{2,18},{10... | collective-permute-start | bytes 393224 | tf_op jit(solution)/shard_map/ppermute | solution.py:38
  33.8 6.4 %collective-permute-start.21 = (f32[4,16,512]{2,1,0:T(8,128)S(1)}, f32[4,16,512]{2,1,0:T(8,128)S(1)}, u32[]{:S(2)}, u32[]{:S(2)}) collective-permute-start(f32[4,16,512]{2,1,0:T(8,128)S(1)} %shard_map.127.refs_0_.refs_4_), channel_id=1, source_target_pairs={{0,8},{8,0},{16,24},{24,16},{1,9},{9,1},{17,25},{25,17},{2,10},{10... | collective-permute-start | bytes 393224 | tf_op jit(solution)/shard_map/ppermute | solution.py:38
  34.7 8.1 %collective-permute-start.6 = (f32[4,16,512]{2,1,0:T(8,128)S(1)}, f32[4,16,512]{2,1,0:T(8,128)S(1)}, u32[]{:S(2)}, u32[]{:S(2)}) collective-permute-start(f32[4,16,512]{2,1,0:T(8,128)S(1)} %shard_map.124.refs_0_.refs_4_), channel_id=1, source_target_pairs={{0,24},{8,16},{16,8},{24,0},{1,25},{9,17},{17,9},{25,1},{2,26},{10... | collective-permute-start | bytes 393224 | tf_op jit(solution)/shard_map/ppermute | solution.py:38
  35.8 7.4 %collective-permute-start.5 = (f32[4,16,512]{2,1,0:T(8,128)S(1)}, f32[4,16,512]{2,1,0:T(8,128)S(1)}, u32[]{:S(2)}, u32[]{:S(2)}) collective-permute-start(f32[4,16,512]{2,1,0:T(8,128)S(1)} %shard_map.124.refs_0_.refs_4_), channel_id=1, source_target_pairs={{0,16},{8,24},{16,0},{24,8},{1,17},{9,25},{17,1},{25,9},{2,18},{10... | collective-permute-start | bytes 393224 | tf_op jit(solution)/shard_map/ppermute | solution.py:38
  37.5 6.5 %collective-permute-start.4 = (f32[4,16,512]{2,1,0:T(8,128)S(1)}, f32[4,16,512]{2,1,0:T(8,128)S(1)}, u32[]{:S(2)}, u32[]{:S(2)}) collective-permute-start(f32[4,16,512]{2,1,0:T(8,128)S(1)} %shard_map.124.refs_0_.refs_4_), channel_id=1, source_target_pairs={{0,8},{8,0},{16,24},{24,16},{1,9},{9,1},{17,25},{25,17},{2,10},{10... | collective-permute-start | bytes 393224 | tf_op jit(solution)/shard_map/ppermute | solution.py:38
  40.3 9.0 %collective-permute-start.26 = (f32[4,16,512]{2,1,0:T(8,128)S(1)}, f32[4,16,512]{2,1,0:T(8,128)S(1)}, u32[]{:S(2)}, u32[]{:S(2)}) collective-permute-start(f32[4,16,512]{2,1,0:T(8,128)S(1)} %get-tuple-element.59.refs_0_), channel_id=1, source_target_pairs={{0,4},{1,5},{2,6},{3,7},{4,0},{5,1},{6,2},{7,3},{8,12},{9,13},{10,... | collective-permute-start | bytes 393224 | tf_op jit(solution)/shard_map/ppermute | solution.py:38
  44.0 9.2 %collective-permute-start.12 = (f32[4,16,512]{2,1,0:T(8,128)S(1)}, f32[4,16,512]{2,1,0:T(8,128)S(1)}, u32[]{:S(2)}, u32[]{:S(2)}) collective-permute-start(f32[4,16,512]{2,1,0:T(8,128)S(1)} %get-tuple-element.50.refs_0_), channel_id=1, source_target_pairs={{0,4},{1,5},{2,6},{3,7},{4,0},{5,1},{6,2},{7,3},{8,12},{9,13},{10,... | collective-permute-start | bytes 393224 | tf_op jit(solution)/shard_map/ppermute | solution.py:38
  45.3 9.6 %collective-permute-start.10 = (f32[4,16,512]{2,1,0:T(8,128)S(1)}, f32[4,16,512]{2,1,0:T(8,128)S(1)}, u32[]{:S(2)}, u32[]{:S(2)}) collective-permute-start(f32[4,16,512]{2,1,0:T(8,128)S(1)} %get-tuple-element.50.refs_0_), channel_id=1, source_target_pairs={{0,2},{1,3},{2,0},{3,1},{4,6},{5,7},{6,4},{7,5},{8,10},{9,11},{10,... | collective-permute-start | bytes 393224 | tf_op jit(solution)/shard_map/ppermute | solution.py:38
  48.5 9.3 %collective-permute-start.24 = (f32[4,16,512]{2,1,0:T(8,128)S(1)}, f32[4,16,512]{2,1,0:T(8,128)S(1)}, u32[]{:S(2)}, u32[]{:S(2)}) collective-permute-start(f32[4,16,512]{2,1,0:T(8,128)S(1)} %get-tuple-element.59.refs_0_), channel_id=1, source_target_pairs={{0,2},{1,3},{2,0},{3,1},{4,6},{5,7},{6,4},{7,5},{8,10},{9,11},{10,... | collective-permute-start | bytes 393224 | tf_op jit(solution)/shard_map/ppermute | solution.py:38
  49.3 10.4 %collective-permute-start.28 = (f32[4,16,512]{2,1,0:T(8,128)S(1)}, f32[4,16,512]{2,1,0:T(8,128)S(1)}, u32[]{:S(2)}, u32[]{:S(2)}) collective-permute-start(f32[4,16,512]{2,1,0:T(8,128)S(1)} %collective-permute-done.26.refs_3_), channel_id=1, source_target_pairs={{0,2},{1,3},{2,0},{3,1},{4,6},{5,7},{6,4},{7,5},{8,10},{9,11},{10,... | collective-permute-start | bytes 393224 | tf_op jit(solution)/shard_map/ppermute | solution.py:38
  51.1 8.6 %collective-permute-start.30 = (f32[4,16,512]{2,1,0:T(8,128)S(1)}, f32[4,16,512]{2,1,0:T(8,128)S(1)}, u32[]{:S(2)}, u32[]{:S(2)}) collective-permute-start(f32[4,16,512]{2,1,0:T(8,128)S(1)} %get-tuple-element.59.refs_0_), channel_id=1, source_target_pairs={{0,1},{1,0},{2,3},{3,2},{4,5},{5,4},{6,7},{7,6},{8,9},{9,8},{10,11... | collective-permute-start | bytes 393224 | tf_op jit(solution)/shard_map/ppermute | solution.py:38
  53.2 7.9 %collective-permute-start.14 = (f32[4,16,512]{2,1,0:T(8,128)S(1)}, f32[4,16,512]{2,1,0:T(8,128)S(1)}, u32[]{:S(2)}, u32[]{:S(2)}) collective-permute-start(f32[4,16,512]{2,1,0:T(8,128)S(1)} %collective-permute-done.12.refs_3_), channel_id=1, source_target_pairs={{0,2},{1,3},{2,0},{3,1},{4,6},{5,7},{6,4},{7,5},{8,10},{9,11},{10,... | collective-permute-start | bytes 393224 | tf_op jit(solution)/shard_map/ppermute | solution.py:38
  54.9 6.2 %collective-permute-start.27 = (f32[4,16,512]{2,1,0:T(8,128)S(1)}, f32[4,16,512]{2,1,0:T(8,128)S(1)}, u32[]{:S(2)}, u32[]{:S(2)}) collective-permute-start(f32[4,16,512]{2,1,0:T(8,128)S(1)} %collective-permute-done.26.refs_3_), channel_id=1, source_target_pairs={{0,1},{1,0},{2,3},{3,2},{4,5},{5,4},{6,7},{7,6},{8,9},{9,8},{10,11... | collective-permute-start | bytes 393224 | tf_op jit(solution)/shard_map/ppermute | solution.py:38
  59.7 4.0 %collective-permute-start.16 = (f32[4,16,512]{2,1,0:T(8,128)S(1)}, f32[4,16,512]{2,1,0:T(8,128)S(1)}, u32[]{:S(2)}, u32[]{:S(2)}) collective-permute-start(f32[4,16,512]{2,1,0:T(8,128)S(1)} %get-tuple-element.50.refs_0_), channel_id=1, source_target_pairs={{0,1},{1,0},{2,3},{3,2},{4,5},{5,4},{6,7},{7,6},{8,9},{9,8},{10,11... | collective-permute-start | bytes 393224 | tf_op jit(solution)/shard_map/ppermute | solution.py:38
  (14 other events, 152.2 us)
